TPU v7x, 256 devices: a whole 4x4x8 slice. The times are simulated.
256 devices in a mesh: gx: 16 (over z_lo, x), gy: 16 (over y, z_hi, core).
Axes of the slice: x: 4, y: 4, z: 8 (z_hi: 2, z_lo: 4; z = z_hi * 4 + z_lo), core: 2. Of those that a mesh axis runs over, the one named last changes fastest.
Arguments:
- features: float32 [16, 128, 256, 128], P(None, 'gx', 'gy'), may hold values from -6 to 6
- conv_weight: float32 [27, 16, 16], replicated, may hold values from -0.3125 to 0.3125
- mix_weight: float32 [2, 16, 16, 16, 432], P(None, None, None, 'gy', 'gx'), may hold values from -1 to 1
Outputs:
- layer_out: float32 [16, 128, 256, 128], P(None, 'gx', 'gy')
All inputs are finite; a program needn't handle non-finite values.
Results may differ from a plain program's by a relative error of at most 0.0001.
Values sent between devices are 32-bit elements; how exact they have to be, the bound alone decides.
A program may use at most 128 MiB of HBM per device.

v0:
```python
import math

import jax
import jax.numpy as jnp
from jax import lax
from jax.sharding import PartitionSpec as P

KX = 24
KY = 24
KZ = 12


PRECISE = lax.Precision.HIGHEST


def padded_2(array, sides, width):
    for axis, dim in sides:
        size, length = (lax.axis_size(axis), array.shape[dim])
        up = [(i, (i + 1) % size) for i in range(size)]
        down = [(j, i) for i, j in up]
        last = lax.slice_in_dim(array, length - width, length, axis=dim)
        initial = lax.slice_in_dim(array, 0, width, axis=dim)
        before = lax.ppermute(last, axis, up)
        after = lax.ppermute(initial, axis, down)
        array = jnp.concatenate([before, array, after], axis=dim)
    return array


def angle_tables(positions, frequencies, length):
    product = positions[:, None] * frequencies[None, :] % length
    angles = product.astype(jnp.float32) * (2.0 * math.pi / length)
    return (jnp.cos(angles), jnp.sin(angles))


def kept_frequencies(amount, length):
    index = jnp.arange(amount, dtype=jnp.int32)
    return jnp.where(index < amount // 2, index, length - amount + index)


def forward_x(part_real, part_imag, cos_x, sin_x):
    out_real = jnp.einsum("cxm,xp->cpm", part_real, cos_x, precision=PRECISE) + jnp.einsum(
        "cxm,xp->cpm", part_imag, sin_x, precision=PRECISE
    )
    out_imag = jnp.einsum("cxm,xp->cpm", part_imag, cos_x, precision=PRECISE) - jnp.einsum(
        "cxm,xp->cpm", part_real, sin_x, precision=PRECISE
    )
    return (out_real, out_imag)


def inverse_x(part_real, part_imag, cos_x, sin_x):
    out_real = jnp.einsum("cpm,xp->cxm", part_real, cos_x, precision=PRECISE) - jnp.einsum(
        "cpm,xp->cxm", part_imag, sin_x, precision=PRECISE
    )
    out_imag = jnp.einsum("cpm,xp->cxm", part_imag, cos_x, precision=PRECISE) + jnp.einsum(
        "cpm,xp->cxm", part_real, sin_x, precision=PRECISE
    )
    return (out_real, out_imag)


def shards(features, conv_weight, mix_weight):
    channels, cells_x, cells_y, length_z = features.shape
    count_gx = lax.axis_size("gx")
    count_gy = lax.axis_size("gy")
    length_x = cells_x * count_gx
    length_y = cells_y * count_gy
    block_yz = KY * KZ // count_gy
    padded = padded_2(features, (("gx", 1), ("gy", 2)), 1)
    wrapped = jnp.concatenate([padded[..., -1:], padded, padded[..., :1]], axis=3)
    kernel = conv_weight.reshape(3, 3, 3, channels, channels).transpose(3, 4, 0, 1, 2)
    conv_sum = lax.conv_general_dilated(
        wrapped[None],
        kernel,
        (1, 1, 1),
        "VALID",
        dimension_numbers=("NCDHW", "OIDHW", "NCDHW"),
        precision=PRECISE,
    )[0]
    cos_z, sin_z = angle_tables(
        jnp.arange(length_z, dtype=jnp.int32), jnp.arange(KZ, dtype=jnp.int32), length_z
    )
    y_places = lax.axis_index("gy") * cells_y + jnp.arange(cells_y, dtype=jnp.int32)
    x_places = lax.axis_index("gx") * cells_x + jnp.arange(cells_x, dtype=jnp.int32)
    cos_y, sin_y = angle_tables(y_places, kept_frequencies(KY, length_y), length_y)
    cos_x, sin_x = angle_tables(x_places, kept_frequencies(KX, length_x), length_x)
    table_z = jnp.concatenate([cos_z, -sin_z], axis=1)
    along_z = jnp.dot(features, table_z, precision=PRECISE)
    z_real = along_z[..., :KZ]
    z_imag = along_z[..., KZ:]
    y_real = jnp.einsum("cxyk,yq->cxqk", z_real, cos_y, precision=PRECISE) + jnp.einsum(
        "cxyk,yq->cxqk", z_imag, sin_y, precision=PRECISE
    )
    y_imag = jnp.einsum("cxyk,yq->cxqk", z_imag, cos_y, precision=PRECISE) - jnp.einsum(
        "cxyk,yq->cxqk", z_real, sin_y, precision=PRECISE
    )
    partial_value = jnp.stack([y_real, y_imag], axis=2).reshape(channels, cells_x, 2, KY * KZ)
    y_share = lax.psum_scatter(partial_value, "gy", scatter_dimension=3, tiled=True)
    x_real, x_imag = forward_x(y_share[:, :, 0], y_share[:, :, 1], cos_x, sin_x)
    x_partial = jnp.stack([x_real, x_imag], axis=1).reshape(channels, 2, KX * block_yz)
    owned_modes = lax.psum_scatter(x_partial, "gx", scatter_dimension=2, tiled=True)
    forward_scale = 1.0 / math.sqrt(length_x * length_y * length_z)
    owned_modes = owned_modes * forward_scale
    coef_real = owned_modes[:, 0]
    coef_imag = owned_modes[:, 1]
    weight_real = mix_weight[0, :, :, 0, :]
    weight_imag = mix_weight[1, :, :, 0, :]
    mixed_real = jnp.einsum("oim,im->om", weight_real, coef_real, precision=PRECISE) - jnp.einsum(
        "oim,im->om", weight_imag, coef_imag, precision=PRECISE
    )
    mixed_imag = jnp.einsum("oim,im->om", weight_real, coef_imag, precision=PRECISE) + jnp.einsum(
        "oim,im->om", weight_imag, coef_real, precision=PRECISE
    )
    mixed_modes = jnp.stack([mixed_real, mixed_imag], axis=1)
    row_modes = lax.all_gather(mixed_modes, "gx", axis=2, tiled=True).reshape(
        channels, 2, KX, block_yz
    )
    back_real, back_imag = inverse_x(row_modes[:, 0], row_modes[:, 1], cos_x, sin_x)
    x_inverse = jnp.stack([back_real, back_imag], axis=2)
    gathered = lax.all_gather(x_inverse, "gy", axis=3, tiled=True)
    back_real = gathered[:, :, 0].reshape(channels, cells_x, KY, KZ)
    back_imag = gathered[:, :, 1].reshape(channels, cells_x, KY, KZ)
    plane_real = jnp.einsum("cxqk,yq->cxyk", back_real, cos_y, precision=PRECISE) - jnp.einsum(
        "cxqk,yq->cxyk", back_imag, sin_y, precision=PRECISE
    )
    plane_imag = jnp.einsum("cxqk,yq->cxyk", back_imag, cos_y, precision=PRECISE) + jnp.einsum(
        "cxqk,yq->cxyk", back_real, sin_y, precision=PRECISE
    )
    table_back = jnp.concatenate([cos_z.T, -sin_z.T], axis=0)
    inverse_scale = 1.0 / math.sqrt(KX * KY * KZ)
    spectral = (
        jnp.dot(jnp.concatenate([plane_real, plane_imag], axis=3), table_back, precision=PRECISE)
        * inverse_scale
    )
    return jax.nn.gelu(conv_sum + spectral, approximate=False)


def solution(mesh):
    in_specs = (P(None, "gx", "gy", None), P(), P(None, None, None, "gy", "gx"))
    out_specs = P(None, "gx", "gy", None)
    return jax.shard_map(shards, mesh=mesh, in_specs=in_specs, out_specs=out_specs, check_vma=False)
```

profile of v0, /device:TPU:7, one launch (start us, length us, event | category | flops | bytes accessed | tf_op | source)
XLA Modules:
  0.0 493.7 jit_solution(6698932705271622397)
XLA Ops:
  6.6 2.2 convolution_bitcast_fusion
  8.8 1.3 fusion.181
  10.1 2.1 copy.51
  12.2 0.9 copy.52
  13.2 0.9 fusion.63
  14.1 0.9 fusion.61
  14.9 1.8 fusion.13
  16.7 2.0 copy.53
  18.7 0.5 stack.36
  19.1 0.9 fusion.12
  20.0 0.8 copy.56
  20.9 0.5 stack.37
  21.4 0.8 pad_maximum_fusion.1
  22.3 1.6 collective-permute-start
  24.1 0.7 dynamic-slice
  24.8 0.6 dynamic-slice.2
  27.0 0.6 constant_dynamic-update-slice_fusion.1
  27.6 2.3 collective-permute-done.1
  30.0 8.1 %collective-permute-start.2 = (f32[16,10,1,128]{3,0,2,1:T(8,128)S(1)}, f32[16,10,1,128]{3,0,2,1:T(8,128)S(1)}, u32[]{:S(2)}, u32[]{:S(2)}) collective-permute-start(f32[16,10,1,128]{3,0,2,1:T(8,128)S(1)} %get-tuple-element.15), channel_id=1, source_target_pairs={{0,1},{1,2},{2,3},{3,4},{4,5},{5,6},{6,7},{7,8},{8,9},{9,10},{10,1... | collective-permute-start | bytes 245768 | tf_op jit(solution)/shard_map/ppermute | solution.py:23
  38.1 0.4 collective-permute-start.3
  38.5 1.0 collective-permute-done.2
  39.5 7.2 %collective-permute-done.3 = f32[16,10,1,128]{3,0,2,1:T(8,128)S(1)} collective-permute-done((f32[16,10,1,128]{3,0,2,1:T(8,128)S(1)}, f32[16,10,1,128]{3,0,2,1:T(8,128)S(1)}, u32[]{:S(2)}, u32[]{:S(2)}) %collective-permute-start.3) | collective-permute-done | bytes 81952 | tf_op jit(solution)/shard_map/ppermute | solution.py:24
  46.8 0.5 fusion.178
  47.3 1.2 maximum_bitcast_fusion
  48.9 6.5 %reshape.44 = f32[16,10,18,1,8,17]{5,4,0,2,1,3:T(8,128)} reshape(f32[16,10,18,1,136]{4,0,2,1,3:T(8,128)S(1)} %pad) | data formatting | bytes 3133440 | tf_op jit(solution)/shard_map/conv_general_dilated | solution.py:70
  55.4 15.0 %copy.47 = f32[16,10,18,1,8,17]{0,4,5,2,1,3:T(8,128)} copy(f32[16,10,18,1,8,17]{5,4,0,2,1,3:T(8,128)} %reshape.44) | data formatting | bytes 3133440 | tf_op jit(solution)/shard_map/conv_general_dilated | solution.py:70
  70.4 1.5 slice.80
  71.9 5.3 %fusion.197 = f32[16,10,18,8,19]{0,3,4,2,1:T(8,128)S(1)} fusion(f32[16,10,18,1,7,2]{0,4,5,2,1,3:T(8,128)S(1)} %slice.80, f32[16,10,18,1,8,17]{0,4,5,2,1,3:T(8,128)} %copy.47), kind=kLoop, calls=%fused_computation.1.clone.clone.clone.clone.1 | loop fusion | flops 1313280 | bytes 3479040 | tf_op jit(solution)/shard_map/conv_general_dilated | solution.py:70
  77.2 193.4 %broadcast_select_fusion = f32[8,16,8,17,16]{4,2,3,1,0:T(8,128)} fusion(pred[8,17]{0,1:T(8,128)(4,1)S(1)} %copy-done.7, f32[3,3,3,16,16]{4,3,2,1,0:T(8,128)S(1)} %bitcast.181, f32[16,10,18,8,19]{0,3,4,2,1:T(8,128)S(1)} %fusion.197), kind=kOutput, calls=%fused_computation.8 | convolution fusion | flops 1444167680 | bytes 2892936 | tf_op jit(solution)/shard_map/conv_general_dilated | solution.py:70
  270.7 12.7 %copy.98 = f32[8,16,8,17,16]{3,2,1,0,4:T(8,128)} copy(f32[8,16,8,17,16]{4,2,3,1,0:T(8,128)} %broadcast_select_fusion) | data formatting | bytes 2228224 | tf_op jit(solution)/shard_map/conv_general_dilated | solution.py:70
  283.4 7.0 %reshape.68 = f32[8,16,1,136,16]{3,1,0,4,2:T(8,128)} reshape(f32[8,16,8,17,16]{3,2,1,0,4:T(8,128)} %copy.98) | data formatting | bytes 2228224 | tf_op jit(solution)/shard_map/conv_general_dilated | solution.py:70
  290.4 1.4 fusion.38
  291.8 1.4 fusion.15
  293.3 1.4 fusion.39
  294.7 1.4 fusion.14
  296.3 57.2 %all-reduce.1 = f32[16,2,432]{2,0,1:T(8,128)S(1)} all-reduce(f32[16,2,432]{2,0,1:T(8,128)S(1)} %pad_maximum_fusion.3), channel_id=3, replica_groups=mesh['gx'=16,'gy'=16] {'gx'}, use_global_device_ids=true, to_apply=%region_1.2.clone | all-reduce | flops 13824 | bytes 110592
  353.8 38.1 %all_gather.6 = f32[16,2,432]{0,1,2:T(2,128)S(1)} all-gather(f32[16,2,27]{0,1,2:T(2,128)S(1)} %copy.57), channel_id=1, replica_groups=mesh['gx'=16,'gy'=16] {'gx'}, dimensions={2}, use_global_device_ids=true | all-gather | bytes 58752 | tf_op jit(solution)/shard_map/all_gather | solution.py:113
  391.8 0.3 fusion.182
  394.2 76.2 %all_gather.7 = f32[16,8,2,288]{0,1,2,3:T(8,128)S(1)} all-gather(f32[16,8,2,18]{0,1,2,3:T(8,128)S(1)} %copy.59), channel_id=1, replica_groups=mesh['gx'=16,'gy'=16] {'gy'}, dimensions={3}, use_global_device_ids=true | all-gather | bytes 313344 | tf_op jit(solution)/shard_map/all_gather | solution.py:118
  470.4 1.2 fusion.177
  471.5 1.7 copy.93
  473.2 2.2 fusion.59
  475.4 2.9 copy.94
  478.3 1.2 fusion.57
  479.5 1.2 fusion.10
  480.7 1.2 fusion.9
  481.9 0.4 copy-done.2
  482.3 4.2 fusion.19
  (54 shorter events, 3.5 us)
Async XLA Ops:
  6.5 283.9 %all-reduce.4.cloned.1.call-start = ((), (), s32[]{:S(2)}) async-start(), calls=%async_computation | async-start | bytes 786432
  20.8 1.3 copy-start
  21.3 2.7 copy-start.3
  21.3 2.8 copy-start.6
  21.3 3.4 copy-start.5
  21.4 4.0 copy-start.4
  22.3 4.7 collective-permute-start
  23.9 6.0 %collective-permute-start.1 = (f32[16,1,16,128]{3,0,2,1:T(8,128)S(1)}, f32[16,1,16,128]{3,0,2,1:T(8,128)S(1)}, u32[]{:S(2)}, u32[]{:S(2)}) collective-permute-start(f32[16,1,16,128]{3,0,2,1:T(8,128)S(1)} %copy.121), channel_id=1, source_target_pairs={{16,0},{32,16},{48,32},{64,48},{80,64},{96,80},{112,96},{128,112},... | collective-permute-start | bytes 393224 | tf_op jit(solution)/shard_map/ppermute | solution.py:24
  30.0 9.6 %collective-permute-start.2 = (f32[16,10,1,128]{3,0,2,1:T(8,128)S(1)}, f32[16,10,1,128]{3,0,2,1:T(8,128)S(1)}, u32[]{:S(2)}, u32[]{:S(2)}) collective-permute-start(f32[16,10,1,128]{3,0,2,1:T(8,128)S(1)} %get-tuple-element.15), channel_id=1, source_target_pairs={{0,1},{1,2},{2,3},{3,4},{4,5},{5,6},{6,7},{7,8},{8,9},{9,10},{10,1... | collective-permute-start | bytes 245768 | tf_op jit(solution)/shard_map/ppermute | solution.py:23
  38.1 8.7 %collective-permute-start.3 = (f32[16,10,1,128]{3,0,2,1:T(8,128)S(1)}, f32[16,10,1,128]{3,0,2,1:T(8,128)S(1)}, u32[]{:S(2)}, u32[]{:S(2)}) collective-permute-start(f32[16,10,1,128]{3,0,2,1:T(8,128)S(1)} %get-tuple-element.16), channel_id=1, source_target_pairs={{1,0},{2,1},{3,2},{4,3},{5,4},{6,5},{7,6},{8,7},{9,8},{10,9},{11,1... | collective-permute-start | bytes 245768 | tf_op jit(solution)/shard_map/ppermute | solution.py:24
  71.9 5.3 %copy-start.7 = (pred[8,17]{0,1:T(8,128)(4,1)S(1)}, pred[8,17]{0,1:T(8,128)(4,1)}, u32[]{:S(2)}) copy-start(pred[8,17]{0,1:T(8,128)(4,1)} %constant.131) | copy-start | bytes 412
  478.3 1.2 copy-start.1
  480.7 1.6 copy-start.2
Sparse Core Ops, SparseCore 0:
  22.3 182.2 all-reduce.3
where the time goes:
time: 503 us; the launch traced here: 494 us
  matrix products  217 us (43%)
  blocking collectives  171 us (34%)
  local copies, waits for them, and re-layouts  61.4 us (12%)
  between operations  15.6 us (3%)
  waiting for transfers between devices  10.6 us (2%)
  starting transfers between devices  10.2 us (2%)
  other arithmetic  7.72 us (2%)
    conv_general_dilated x1, matrix products, shards(): lax.conv_general_dilated(wrapped[None], kernel, (1, 1, 1), 'VALID', dimen...  193 us
    all_gather x1, blocking collectives, shards(): gathered = lax.all_gather(x_inverse, 'gy', axis=3, tiled=True)  76.2 us
    unnamed x1, blocking collectives  57.2 us
    conv_general_dilated x5, local copies, waits for them, and re-layouts, shards(): lax.conv_general_dilated(wrapped[None], kernel, (1, 1, 1), 'VALID', dimen...  42.8 us
    all_gather x1, blocking collectives, shards(): lax.all_gather(mixed_modes, 'gx', axis=2, tiled=True)  38.1 us
  transfers between devices with their start and end apart: 5, of which 3 were waited for; matrix products, arithmetic and copies ran while one was open for 50% of the time, Pallas kernels for 0%

commit v1 on v0

v1 whole, which is shorter than its diff:
```python
import functools
import math

import jax
import jax.numpy as jnp
import numpy as np
from jax import lax
from jax.experimental import pallas as pl
from jax.experimental.pallas import tpu as pltpu
from jax.sharding import PartitionSpec as P

C, NX, NY, NZ = 16, 128, 256, 128
KX, KY, KZ = 24, 24, 12
F32, BF16 = jnp.float32, jnp.bfloat16
MESH = pl.DeviceIdType.MESH

PAIRS_B, PAIRS_C, PAIRS_D = 3, 6, 8


def split(a):
    hi = round_bf16(a)
    return hi, round_bf16(np.asarray(a, np.float64) - hi)


def round_bf16(a):
    import ml_dtypes

    return np.asarray(a, np.float32).astype(ml_dtypes.bfloat16).astype(np.float64)


def bf(a):
    import ml_dtypes

    return np.asarray(a, np.float32).astype(ml_dtypes.bfloat16)


def angles(positions, frequencies, length):
    return 2.0 * math.pi * ((positions[:, None] * frequencies[None, :]) % length) / length


def kept(amount, length):
    index = np.arange(amount)
    return np.where(index < amount // 2, index, length - amount + index)


def tables():
    forward = 1.0 / math.sqrt(NX * NY * NZ)
    inverse = 1.0 / math.sqrt(KX * KY * KZ)
    az = angles(np.arange(NZ), np.arange(KZ), NZ).T
    tz = np.stack([np.cos(az), -np.sin(az)], 1).reshape(2 * KZ, NZ)
    hi, lo = split(tz * forward)
    tzf = np.concatenate([hi, lo, hi], 1)
    pad = np.zeros((8, NZ))
    hi, lo = split(np.concatenate([tz * inverse, pad], 0))
    tzi = np.concatenate([hi, lo, hi], 0)

    qs = kept(KY, NY)
    lyf = np.zeros((16, 96, 96))
    lyi = np.zeros((16, 64, 144))
    for gy in range(16):
        fwd = np.zeros((2, 2, KY, 2, 2, 8))
        inv = np.zeros((2, 2, 2, 8, 2, KY))
        for own in range(2):
            start = 16 * (gy if own == 0 else gy ^ 1)
            for yp in range(2):
                a = angles(start + 2 * np.arange(8) + yp, qs, NY)
                c, s = np.cos(a), np.sin(a)
                fwd[yp, 0, :, own, 0] = c.T
                fwd[yp, 0, :, own, 1] = s.T
                fwd[yp, 1, :, own, 0] = -s.T
                fwd[yp, 1, :, own, 1] = c.T
                re = (c, -s)
                im = (s, c)
                for v in range(2):
                    w = v if yp == 0 else 1 - v
                    inv[yp, 0, own, :, v] = re[w]
                    inv[yp, 1, own, :, v] = im[w]
        hi, lo = split(fwd.reshape(96, 32))
        lyf[gy] = np.concatenate([hi, lo, hi], 1)
        hi, lo = split(inv.reshape(64, 48))
        lyi[gy] = np.concatenate([hi, lo, hi], 1)

    ax = angles(np.arange(NX), kept(KX, NX), NX).reshape(16, 8, KX)
    c = np.broadcast_to(np.cos(ax).transpose(0, 2, 1)[:, :, None, :], (16, KX, 8, 8)).reshape(16, KX, 64)
    s = np.broadcast_to(np.sin(ax).transpose(0, 2, 1)[:, :, None, :], (16, KX, 8, 8)).reshape(16, KX, 64)
    tx = np.stack([np.concatenate([c, s], 2), np.concatenate([-s, c], 2)], 0)

    core, ri, ch, x = np.unravel_index(np.arange(256), (2, 2, 8, 8))
    o, i = np.unravel_index(np.arange(256), (16, 16))
    e1 = (i[None, :] == (core * 8 + ch)[:, None]).astype(np.float64)
    e2 = (o[:, None] == (core * 8 + ch)[None, :]).astype(np.float64)
    i128 = np.arange(128) // 8
    ecol = (np.arange(16)[:, None] == i128[None, :]).astype(np.float64)
    xo = np.arange(8)[:, None]
    xi = (np.arange(128) % 8)[None, :]
    mask = np.stack([(xi - xo == a - 1) for a in range(3)], 0).astype(np.float32)
    eh = np.zeros((2, 16, 128))
    mh = np.zeros((2, 8, 128), np.float32)
    for part, (hi_lo) in enumerate("hlh"):
        for side in range(2):
            lanes = part * 32 + side * 16 + np.arange(16)
            eh[0 if hi_lo == "h" else 1, np.arange(16), lanes] = 1.0
            mh[side, 0 if side == 0 else 7, lanes] = 1.0
    return dict(
        tzf=bf(tzf), tzi=bf(tzi), lyf=bf(lyf), lyi=bf(lyi), tx=tx.astype(np.float32), e1=bf(e1), e2=bf(e2),
        ecol=bf(ecol), eh=bf(eh), mask=mask, mh=mh, eye=np.eye(32, 27, dtype=np.float32),
    )


TABLES = tables()
NAMES = ("tzf", "tzi", "lyf", "lyi", "tx", "e1", "e2", "ecol", "eh", "mask", "mh", "eye")
SMALL = ("tzf", "tzi", "tx", "e1", "e2", "ecol", "eh", "mask", "mh", "eye")


def hilo(v):
    hi = v.astype(BF16)
    return hi, (v - hi.astype(F32)).astype(BF16)


def mm(a, b, dims=(((1,), (0,)), ((), ()))):
    return lax.dot_general(a, b, dims, preferred_element_type=F32)


def erf(x):
    x = jnp.clip(x, -3.832506856900711, 3.832506856900711)
    t = x * x
    p = 0.00022905065861350646
    for coef in (0.0034082910107109506, 0.050955695062380861, 0.18520832239976145, 1.128379143519084):
        p = p * t + coef
    q = -1.1791602954361697e-7
    for coef in (0.000023547966471313185, 0.0010179625278914885, 0.014070470171167667, 0.11098505178285362,
                 0.49746925110067538, 1.0):
        q = q * t + coef
    return x * p / q


def gelu(v):
    return 0.5 * v * (1.0 + erf(v * 0.7071067811865476))


def kernel(f2, f3, w_hbm, cw, tzf, tzi, lyf, lyi, tx, e1, e2, ecol, eh, mask, mh, eye, out_hbm, *refs):
    (fv, wv, cwv, tzf_v, tzi_v, tx_v, e1_v, e2_v, ecol_v, eh_v, mask_v, mh_v, eye_v, lyf_v, lyi_v,
     ws, wb, b, lhs, yh_s, yh, xh, cs, ch, za, zr, ps, pr, rs, rb, co_s, rc, g3, u, ur, co, outv,
     ld, a_s, a_r, h_s, h_r, y_s, y_r, b_s, b_r, c_s, c_r, d_s, d_r, w_s, w_r, u_s, u_r) = refs
    gx = lax.axis_index("gx")
    gy = lax.axis_index("gy")
    y = gy // 4
    jj = gy % 4
    s = gy % 2
    me = gx * 4 + jj
    gxm, gxp = (gx + 15) % 16, (gx + 1) % 16
    gym, gyp = (gy + 15) % 16, (gy + 1) % 16

    loads = [(f2, fv), (w_hbm, wv), (cw, cwv), (lyf.at[gy], lyf_v), (lyi.at[gy], lyi_v), (tzf, tzf_v), (tzi, tzi_v),
             (tx, tx_v), (e1, e1_v), (e2, e2_v), (ecol, ecol_v), (eh, eh_v), (mask, mask_v), (mh, mh_v), (eye, eye_v)]
    copies = [pltpu.make_async_copy(src, dst, ld.at[n]) for n, (src, dst) in enumerate(loads)]
    for copy in copies:
        copy.start()

    barrier = pltpu.get_barrier_semaphore()

    def greet(d, carry):
        @pl.when(d != me)
        def _():
            pl.semaphore_signal(barrier, inc=1, device_id=(d // 4, y * 4 + d % 4), device_id_type=MESH)
        return carry

    lax.fori_loop(0, 64, greet, 0)
    for step in range(1, 4):
        pl.semaphore_signal(barrier, inc=1, device_id=(gx, (gy + 4 * step) % 16), device_id_type=MESH)
    for px in (gxm, gx, gxp):
        for py in (gym, gyp):
            pl.semaphore_signal(barrier, inc=1, device_id=(px, py), device_id_type=MESH)

    b[384:512, :] = jnp.zeros((128, 18 * 128), BF16)
    copies[0].wait()
    for yy in range(16):
        a = jnp.concatenate([fv[pl.ds(c * 128 + yy, 8, stride=16), :] for c in range(16)], 0)
        hi, lo = hilo(a)
        lanes = slice((yy + 1) * 128, (yy + 2) * 128)
        b[0:128, lanes] = hi
        b[128:256, lanes] = lo
        b[256:384, lanes] = hi
        if yy in (0, 15):
            yh_s[0 if yy == 0 else 1] = a
    for n, (x0, y0) in enumerate(((0, 0), (0, 15), (7, 0), (7, 15))):
        cs[n] = jnp.concatenate([fv[pl.ds(c * 128 + x0 * 16 + y0, 1), :] for c in range(16)], 0)

    copies[5].wait()
    for h in range(2):
        for yy in range(8):
            l0 = (2 * yy + 1) * 128
            rows = slice(h * 64, h * 64 + 64)
            lrow = slice(128 + h * 64, 128 + h * 64 + 64)
            hi = jnp.concatenate([b[rows, l0:l0 + 128], b[rows, l0 + 128:l0 + 256]], 0)
            lo = jnp.concatenate([b[lrow, l0:l0 + 128], b[lrow, l0 + 128:l0 + 256]], 0)
            r = mm(tzf_v[...], jnp.concatenate([hi, hi, lo], 1), (((1,), (1,)), ((), ())))
            za[h, pl.ds(yy, 24, stride=8), :] = r

    pl.semaphore_wait(barrier, 72)

    def remote(src, dst, ssem, rsem, px, py):
        return pltpu.make_async_remote_copy(src_ref=src, dst_ref=dst, send_sem=ssem, recv_sem=rsem,
                                            device_id=(px, py), device_id_type=MESH)

    partner = jj + 1 - 2 * s + 4 * y
    ca = remote(za.at[1 - s], zr, a_s, a_r, gx, partner)
    ca.start()

    copies[1].wait()
    copies[14].wait()
    for n in range(4):
        t = lax.dot_general(eye_v[...], wv[pl.ds(128 * n, 128), :], (((1,), (1,)), ((), ())),
                            precision=lax.Precision.HIGHEST, preferred_element_type=F32)
        for m in range(27):
            ws[m, n, :] = t[m, :]

    def owner(r):
        double = r // 64
        return (r - 64 * double) * (1 + 7 * double), double

    def w_copy(m):
        mode = 27 * gx + m
        d, slot = owner(18 * jj + mode % 18)
        p = mode // 18
        return d, slot, p, remote(ws.at[m], wb.at[slot, p], w_s.at[m], w_r.at[slot], d // 4, y * 4 + d % 4)

    def w_send(m, carry):
        d, slot, p, copy = w_copy(m)

        @pl.when(d != me)
        def _():
            copy.start()

        @pl.when(d == me)
        def _():
            pltpu.make_async_copy(ws.at[m], wb.at[slot, p], w_r.at[slot]).start()
        return carry

    lax.fori_loop(0, 27, w_send, 0)

    halos = [
        remote(f3.at[:, pl.ds(112, 16), :], xh.at[0], h_s.at[0], h_r.at[0], gxp, gy),
        remote(f3.at[:, pl.ds(0, 16), :], xh.at[1], h_s.at[1], h_r.at[1], gxm, gy),
        remote(yh_s.at[1], yh.at[0], h_s.at[2], h_r.at[2], gx, gyp),
        remote(yh_s.at[0], yh.at[1], h_s.at[3], h_r.at[3], gx, gym),
        remote(cs.at[0], ch.at[3], h_s.at[4], h_r.at[7], gxm, gym),
        remote(cs.at[1], ch.at[2], h_s.at[5], h_r.at[6], gxm, gyp),
        remote(cs.at[2], ch.at[1], h_s.at[6], h_r.at[5], gxp, gym),
        remote(cs.at[3], ch.at[0], h_s.at[7], h_r.at[4], gxp, gyp),
    ]
    for copy in halos:
        copy.start()

    copies[3].wait()
    ca.wait_recv()
    half = lax.broadcasted_iota(jnp.int32, (24, 128), 1) < 64
    for k in range(12):
        v = jnp.concatenate([za[s, 16 * k:16 * k + 16, :], zr[16 * k:16 * k + 16, :]], 0)
        hi, lo = hilo(v)
        r = mm(lyf_v[...], jnp.concatenate([hi, hi, lo], 0))
        p0 = jnp.where(half, r[0:24], r[72:96])
        p1 = jnp.where(half, r[24:48], r[48:72])
        ps[pl.ds(k, 24, stride=12), :] = p0 + pltpu.roll(p1, 64, 1)

    ycopies = []
    for step in (1, 2, 3):
        yt = (y + step) % 4
        copy = remote(ps.at[pl.ds(pl.multiple_of(yt * 72, 8), 72), :], pr.at[step - 1], y_s.at[step - 1],
                      y_r.at[step - 1], gx, yt * 4 + jj)
        copy.start()
        ycopies.append(copy)
    for n in (2, 10, 11, 12, 13):
        copies[n].wait()
    whi, wlo = hilo(cwv[...])
    ecol_m = ecol_v[...]
    x_hi = mm(whi, ecol_m)
    x_lo = mm(wlo, ecol_m)
    x_h = mm(whi, eh_v[0]) + mm(wlo, eh_v[1])
    masks = [mask_v[a][None] for a in range(3)]

    def spread(v, m, taps):
        total = None
        for t, a in taps:
            term = v[144 * a:144 * a + 144][:, None, :] * m[t]
            total = term if total is None else total + term
        return total.reshape(1152, 128).astype(BF16)

    taps = ((0, 0), (1, 1), (2, 2))
    full_hi = spread(x_hi, masks, taps)
    lhs[:, 0:128] = full_hi
    lhs[:, 128:256] = full_hi
    lhs[:, 256:384] = spread(x_lo, masks, taps)
    lhs[:, 384:512] = spread(x_h, [mh_v[a][None] for a in range(2)], ((0, 0), (1, 2)))

    for copy in ycopies:
        copy.wait_recv()
    own = ps[pl.ds(pl.multiple_of(y * 72, 8), 72), :]
    total = own + pr[0] + pr[1] + pr[2]
    for r in range(72):
        rs[r, :, :] = total[r:r + 1, :]

    def b_send(r, carry):
        d, slot = owner(r)

        @pl.when(d != me)
        def _():
            remote(rs.at[r], rb.at[slot, me], b_s, b_r.at[slot], d // 4, y * 4 + d % 4).start()

        @pl.when(d == me)
        def _():
            pltpu.make_async_copy(rs.at[r], rb.at[slot, me], b_r.at[slot]).start()
        return carry

    lax.fori_loop(0, 72, b_send, 0)
    double = me % 8 == 0

    for copy in halos:
        copy.wait_recv()
    ring = [(0, 0), (17, 1)]
    for yi, side in ring:
        hi, lo = hilo(yh[side])
        lanes = slice(yi * 128, yi * 128 + 128)
        b[0:128, lanes] = hi
        b[128:256, lanes] = lo
        b[256:384, lanes] = hi
    for yi in range(18):
        if yi == 0:
            v = jnp.concatenate([ch[0], ch[2]], 0)
        elif yi == 17:
            v = jnp.concatenate([ch[1], ch[3]], 0)
        else:
            v = jnp.concatenate([xh[side, c, pl.ds(yi - 1, 1), :] for side in range(2) for c in range(16)], 0)
        hi, lo = hilo(v)
        b[384:480, yi * 128:yi * 128 + 128] = jnp.concatenate([hi, hi, lo], 0)

    def conv(pair, carry):
        acc = jnp.zeros((384, 256), F32)
        for t in range(3):
            lanes = pl.ds(pl.multiple_of((2 * pair + t) * 128, 128), 256)
            acc = acc + mm(lhs[384 * t:384 * t + 384, :], b[:, lanes])
        for n in range(2):
            v = acc[:, 128 * n:128 * n + 128]
            v = v[128:256] + pltpu.roll(v[0:128], 1, 1) + pltpu.roll(v[256:384], 127, 1)
            co[pl.ds(pl.multiple_of((2 * pair + n) * 128, 128), 128), :] = v
        return carry

    lax.fori_loop(0, PAIRS_B, conv, 0)

    for n in (7, 8, 9):
        copies[n].wait()

    def mix(slot):
        pltpu.make_async_copy(rb.at[slot], rb.at[slot], b_r.at[slot]).wait()
        pltpu.make_async_copy(wb.at[slot], wb.at[slot], w_r.at[slot]).wait()
        accs = [[jnp.zeros((24, 128), F32) for _ in range(2)] for _ in range(2)]
        for g in range(16):
            for core in range(2):
                row = rb[slot, 4 * g + core] + rb[slot, 4 * g + core + 2]
                row = jnp.broadcast_to(row, (24, 128))
                for part in range(2):
                    accs[part][core] = accs[part][core] + tx_v[part, g] * row
        acc = jnp.concatenate([jnp.concatenate(accs[part], 1) for part in range(2)], 0)
        hi, lo = hilo(acc)
        cc = mm(jnp.concatenate([hi, lo], 0), e1_v[...])
        cc = cc[0:48] + cc[48:96]
        cr, ci = cc[0:24], cc[24:48]
        w4 = [jnp.concatenate([wb[slot, p, pl.ds(n, 1), :] for p in range(24)], 0) for n in range(4)]
        wr = jnp.concatenate(w4[0:2], 1)
        wi = jnp.concatenate(w4[2:4], 1)
        prod = jnp.concatenate([wr * cr - wi * ci, wr * ci + wi * cr], 0)
        hi, lo = hilo(prod)
        mx = mm(jnp.concatenate([hi, lo], 0), e2_v[...])
        mx = mx[0:48] + mx[48:96]
        for core in range(2):
            mr = mx[0:24, 128 * core:128 * core + 128]
            mi = mx[24:48, 128 * core:128 * core + 128]
            for g in range(16):
                row = tx_v[0, g] * mr + tx_v[1, g] * mi
                co_s[slot, 2 * g + core] = jnp.sum(row, axis=0, keepdims=True)

        def c_send(d, carry):
            r = me + slot * 64 if slot == 0 else 64 + me // 8

            @pl.when(d != me)
            def _():
                remote(co_s.at[slot, 2 * (d // 4) + d % 2], rc.at[r], c_s.at[slot], c_r, d // 4,
                       y * 4 + d % 4).start()

            @pl.when(d == me)
            def _():
                pltpu.make_async_copy(co_s.at[slot, 2 * (d // 4) + d % 2], rc.at[r], c_r).start()
            return carry

        lax.fori_loop(0, 64, c_send, 0)

    mix(0)

    @pl.when(double)
    def _():
        mix(1)

    lax.fori_loop(PAIRS_B, PAIRS_C, conv, 0)

    pltpu.make_async_copy(rc, rc, c_r).wait()
    for r in range(72):
        g3[0, r:r + 1, :] = rc[r]
    dcopies = []
    for step in (1, 2, 3):
        yt = (y + step) % 4
        copy = remote(g3.at[0], g3.at[4 - step], d_s.at[step - 1], d_r.at[4 - step], gx, yt * 4 + jj)
        copy.start()
        dcopies.append(copy)
    lax.fori_loop(PAIRS_C, PAIRS_D, conv, 0)
    copies[4].wait()
    for n in range(1, 4):
        pltpu.make_async_copy(g3.at[n], g3.at[n], d_r.at[n]).wait()

    half16 = lax.broadcasted_iota(jnp.int32, (16, 128), 1) < 64
    u[:, :, 24:32, :] = jnp.zeros((2, 8, 8, 128), F32)
    for k in range(12):
        v = jnp.concatenate([g3[(t - y) % 4, pl.ds(k, 6, stride=12), :] for t in range(4)], 0)
        v = jnp.concatenate([v, pltpu.roll(v, 64, 1)], 0)
        hi, lo = hilo(v)
        r = mm(lyi_v[...], jnp.concatenate([hi, hi, lo], 0))
        for part in range(2):
            v = jnp.where(half16, r[16 * part:16 * part + 16], r[32 + 16 * part:48 + 16 * part])
            for dst in range(2):
                for yy in range(8):
                    u[dst, yy, pl.ds(2 * k + part, 1), :] = v[8 * dst + yy:8 * dst + yy + 1]

    cu = remote(u.at[1], ur, u_s, u_r, gx, partner)
    cu.start()

    copies[6].wait()

    def finish(v, hh, yy):
        hi, lo = hilo(v)
        r = mm(jnp.concatenate([hi, hi, lo], 0), tzi_v[...], (((0,), (0,)), ((), ())))
        for yp in range(2):
            yr = 2 * yy + yp
            base = pl.multiple_of(yr * 128 + hh * 64, 64)
            t = gelu(r[64 * yp:64 * yp + 64] + co[pl.ds(base, 64), :])
            for c in range(8):
                outv[pl.ds(hh * 1024 + c * 128 + yr, 8, stride=16), :] = t[8 * c:8 * c + 8]

    for yy in range(8):
        finish(u[0, yy], s, yy)
    cu.wait_recv()
    for yy in range(8):
        finish(ur[yy], 1 - s, yy)
    store = pltpu.make_async_copy(outv, out_hbm, ld.at[15])
    store.start()

    ca.wait_send()
    cu.wait_send()
    for copy in halos + ycopies + dcopies:
        copy.wait_send()

    def w_done(m, carry):
        d, slot, p, copy = w_copy(m)

        @pl.when(d != me)
        def _():
            copy.wait_send()
        return carry

    lax.fori_loop(0, 27, w_done, 0)

    def sent(sem, rows):
        part = rs.at[pl.ds(0, rows)]
        pltpu.make_async_copy(part, part, sem).wait()

    @pl.when(double)
    def _():
        sent(b_s, 70)
        sent(c_s.at[1], 63)

    @pl.when(jnp.logical_not(double))
    def _():
        sent(b_s, 71)

    sent(c_s.at[0], 63)
    store.wait()


def shards(features, conv_weight, mix_weight):
    f2 = features.reshape(2048, 128)
    f3 = features.reshape(16, 128, 128)
    w = mix_weight.reshape(512, 27)
    cw = conv_weight.reshape(432, 16)
    consts = [jnp.asarray(TABLES[n]) for n in NAMES]
    vm = pltpu.VMEM
    dma = pltpu.SemaphoreType.DMA
    scratch = [
        vm((2048, 128), F32), vm((512, 27), F32), vm((432, 16), F32),
        vm((24, 384), BF16), vm((96, 128), BF16), vm((2, 16, 24, 128), F32), vm((256, 256), BF16), vm((256, 256), BF16),
        vm((16, 128), BF16), vm((2, 16, 128), BF16), vm((3, 8, 128), F32), vm((2, 8, 128), F32), vm((32, 27), F32),
        vm((96, 96), BF16), vm((64, 144), BF16),
        vm((27, 4, 128), F32), vm((2, 24, 4, 128), F32), vm((512, 18 * 128), BF16), vm((1152, 512), BF16),
        vm((2, 128, 128), F32), vm((2, 128, 128), F32), vm((2, 16, 16, 128), F32), vm((4, 16, 128), F32),
        vm((4, 16, 128), F32), vm((2, 192, 128), F32), vm((192, 128), F32), vm((288, 128), F32), vm((3, 72, 128), F32),
        vm((72, 1, 128), F32), vm((2, 64, 1, 128), F32), vm((2, 32, 1, 128), F32), vm((72, 1, 128), F32),
        vm((4, 72, 128), F32), vm((2, 8, 32, 128), F32), vm((8, 32, 128), F32), vm((2048, 128), F32),
        vm((2048, 128), F32),
        dma((16,)), dma, dma, dma((8,)), dma((8,)), dma((3,)), dma((3,)), dma, dma((2,)), dma((2,)), dma,
        dma((3,)), dma((4,)), dma((27,)), dma((2,)), dma, dma,
    ]
    any_spec = pl.BlockSpec(memory_space=pl.ANY)
    out = pl.pallas_call(
        kernel,
        out_shape=jax.ShapeDtypeStruct((2048, 128), F32),
        in_specs=[any_spec] * (4 + len(NAMES)),
        out_specs=any_spec,
        scratch_shapes=scratch,
        compiler_params=pltpu.CompilerParams(collective_id=0, has_side_effects=True,
                                             vmem_limit_bytes=56 * 1024 * 1024),
        name="layer",
    )(f2, f3, w, cw, *consts)
    return out.reshape(features.shape)


def solution(mesh):
    in_specs = (P(None, "gx", "gy", None), P(), P(None, None, None, "gy", "gx"))
    return jax.shard_map(shards, mesh=mesh, in_specs=in_specs, out_specs=P(None, "gx", "gy", None), check_vma=False)
```

time: 503 us -> 47.2 us (0.09)
  the two profiles are of different devices: /device:TPU:7 before, /device:TPU:1 now
where the time goes in v1:
time: 47.2 us; the launch traced here: 47 us
  Pallas kernels  43 us (91%)
  local copies, waits for them, and re-layouts  4.06 us (9%)
    pallas_call x1, Pallas kernels, shards(): pl.pallas_call(kernel, out_shape=jax.ShapeDtypeStruct((2048, 128), F32),...  43 us
    unnamed x2, local copies, waits for them, and re-layouts  4.06 us

profile of v1, /device:TPU:1, one launch (start us, length us, event | category | flops | bytes accessed | tf_op | source)
XLA Modules:
  0.0 47.0 jit_solution(8939065821952451528)
XLA Ops:
  0.0 1.8 %copy.16 = f32[27,16,16]{2,1,0:T(8,128)} copy(f32[27,16,16]{0,2,1:T(8,128)} %param.16) | data formatting | bytes 55296 | tf_op args[1]
  1.8 43.0 %layer.1 = f32[2048,128]{1,0:T(8,128)} custom-call(f32[2048,128]{1,0:T(8,128)} %bitcast.5, f32[16,128,128]{2,1,0:T(8,128)} %bitcast.6, f32[512,27]{1,0:T(8,128)} %bitcast.9, f32[432,16]{1,0:T(8,128)} %bitcast.8, bf16[24,384]{1,0:T(8,128)(2,1)} %constant.24.clone.tzf, bf16[96,128]{1,0:T(8,128)(2,1)} %constant.25.clone.tzi, ...), custom_call_target="tpu_custom_call" | custom-call | tf_op jit(solution)/shard_map/layer/pallas_call | solution.py:510
  44.7 2.3 %copy.18 = f32[16,8,16,128]{3,2,1,0:T(8,128)} copy(f32[16,8,16,128]{3,2,1,0:T(8,128)} %bitcast.7) | data formatting | bytes 2097152

commit v2 on v1

v2 whole, which is shorter than its diff:
```python
import functools
import math

import jax
import jax.numpy as jnp
import numpy as np
from jax import lax
from jax.experimental import pallas as pl
from jax.experimental.pallas import tpu as pltpu
from jax.sharding import PartitionSpec as P

C, NX, NY, NZ = 16, 128, 256, 128
KX, KY, KZ = 24, 24, 12
F32, BF16 = jnp.float32, jnp.bfloat16
MESH = pl.DeviceIdType.MESH


def split(a):
    hi = round_bf16(a)
    return hi, round_bf16(np.asarray(a, np.float64) - hi)


def round_bf16(a):
    import ml_dtypes

    return np.asarray(a, np.float32).astype(ml_dtypes.bfloat16).astype(np.float64)


def bf(a):
    import ml_dtypes

    return np.asarray(a, np.float32).astype(ml_dtypes.bfloat16)


def angles(positions, frequencies, length):
    return 2.0 * math.pi * ((positions[:, None] * frequencies[None, :]) % length) / length


def kept(amount, length):
    index = np.arange(amount)
    return np.where(index < amount // 2, index, length - amount + index)


def tables():
    forward = 1.0 / math.sqrt(NX * NY * NZ)
    inverse = 1.0 / math.sqrt(KX * KY * KZ)
    az = angles(np.arange(NZ), np.arange(KZ), NZ).T
    tz = np.stack([np.cos(az), -np.sin(az)], 1).reshape(2 * KZ, NZ)
    hi, lo = split(tz * forward)
    tzf = np.concatenate([hi, lo, hi], 1)
    pad = np.zeros((8, NZ))
    hi, lo = split(np.concatenate([tz * inverse, pad], 0))
    tzi = np.concatenate([hi, lo, hi], 0)

    qs = kept(KY, NY)
    lyf = np.zeros((16, 96, 96))
    lyi = np.zeros((16, 64, 192))
    for gy in range(16):
        fwd = np.zeros((2, 2, KY, 2, 2, 8))
        inv = np.zeros((2, 2, 2, 8, 2, KY))
        for own in range(2):
            start = 16 * (gy if own == 0 else gy ^ 1)
            for yp in range(2):
                a = angles(start + 2 * np.arange(8) + yp, qs, NY)
                c, s = np.cos(a), np.sin(a)
                fwd[yp, 0, :, own, 0] = c.T
                fwd[yp, 0, :, own, 1] = s.T
                fwd[yp, 1, :, own, 0] = -s.T
                fwd[yp, 1, :, own, 1] = c.T
                re = (c, -s)
                im = (s, c)
                for v in range(2):
                    w = v if yp == 0 else 1 - v
                    inv[yp, 0, own, :, v] = re[w]
                    inv[yp, 1, own, :, v] = im[w]
        hi, lo = split(fwd.reshape(96, 32))
        lyf[gy] = np.concatenate([hi, lo, hi], 1)
        inv = np.concatenate([inv.reshape(64, 2, 4, 6), np.zeros((64, 2, 4, 2))], 3)
        hi, lo = split(inv.reshape(64, 64))
        lyi[gy] = np.concatenate([hi, lo, hi], 1)

    ax = angles(np.arange(NX), kept(KX, NX), NX).reshape(16, 8, KX)
    c = np.broadcast_to(np.cos(ax).transpose(0, 2, 1)[:, :, None, :], (16, KX, 8, 8)).reshape(16, KX, 64)
    s = np.broadcast_to(np.sin(ax).transpose(0, 2, 1)[:, :, None, :], (16, KX, 8, 8)).reshape(16, KX, 64)
    tx = np.stack([np.concatenate([c, s], 2), np.concatenate([-s, c], 2)], 0)

    core, ri, ch, x = np.unravel_index(np.arange(256), (2, 2, 8, 8))
    o, i = np.unravel_index(np.arange(256), (16, 16))
    e1 = (i[None, :] == (core * 8 + ch)[:, None]).astype(np.float64)
    e2 = (o[:, None] == (core * 8 + ch)[None, :]).astype(np.float64)
    i128 = np.arange(128) // 8
    ecol = (np.arange(256)[:, None] % 16 == i128[None, :]).astype(np.float64)
    xo = np.arange(8)[:, None]
    xi = (np.arange(128) % 8)[None, :]
    mask = np.stack([(xi - xo == a - 1) for a in range(3)], 0).astype(np.float32)
    eh = np.zeros((2, 256, 128))
    mh = np.zeros((3, 8, 128), np.float32)
    for part, (hi_lo) in enumerate("hlh"):
        for side in range(2):
            lanes = part * 32 + side * 16 + np.arange(16)
            eh[0 if hi_lo == "h" else 1, np.arange(256), lanes[np.arange(256) % 16]] = 1.0
            mh[2 * side, 0 if side == 0 else 7, lanes] = 1.0
    return dict(
        tzf=bf(tzf), tzi=bf(tzi), lyf=bf(lyf), lyi=bf(lyi), tx=tx.astype(np.float32), e1=bf(e1), e2=bf(e2),
        ecol=bf(ecol), eh=bf(eh), mask=mask, mh=mh, eye=np.eye(32, 27, dtype=np.float32),
    )


TABLES = tables()
NAMES = ("tzf", "tzi", "lyf", "lyi", "tx", "e1", "e2", "ecol", "eh", "mask", "mh", "eye")


def hilo(v):
    hi = v.astype(BF16)
    return hi, (v - hi.astype(F32)).astype(BF16)


def mm(a, b, dims=(((1,), (0,)), ((), ()))):
    return lax.dot_general(a, b, dims, preferred_element_type=F32)


def erf(x):
    x = jnp.clip(x, -3.832506856900711, 3.832506856900711)
    t = x * x
    p = 0.00022905065861350646
    for coef in (0.0034082910107109506, 0.050955695062380861, 0.18520832239976145, 1.128379143519084):
        p = p * t + coef
    q = -1.1791602954361697e-7
    for coef in (0.000023547966471313185, 0.0010179625278914885, 0.014070470171167667, 0.11098505178285362,
                 0.49746925110067538, 1.0):
        q = q * t + coef
    return x * p / q


def gelu(v):
    return 0.5 * v * (1.0 + erf(v * 0.7071067811865476))


FAR_Z = (4, 3, 5, 2, 6, 1, 7, 0)
FAR_X = (2, 1, 3, 0)


def kernel(f2, f3, w_hbm, cw, tzf, tzi, lyf, lyi, tx, e1, e2, ecol, eh, mask, mh, eye, v_out, *refs):
    (fv, wv, cwv, tzf_v, tzi_v, tx_v, e1_v, e2_v, ecol_v, eh_v, mask_v, mh_v, eye_v, lyf_v, lyi_v,
     ws, wb, b, lhs, xs, yh_s, yh, xh, cs, ch, za, zr, ps, pr, rs, rb, co_s, rc, g3, u, ur,
     ld, a_s, a_r, h_s, h_r, y_s, y_r, b_s, b_r, c_s, c_r, d_s, d_r, w_s, w_r, u_s, u_r) = refs
    gx = lax.axis_index("gx")
    gy = lax.axis_index("gy")
    y = gy // 4
    jj = gy % 4
    s = gy % 2
    x = gx % 4
    z = (gx // 4) + 4 * (jj // 2)
    me = gx * 4 + jj
    gxm, gxp = (gx + 15) % 16, (gx + 1) % 16
    gym, gyp = (gy + 15) % 16, (gy + 1) % 16

    loads = [(f2, fv), (w_hbm, wv), (cw, cwv), (lyf.at[gy], lyf_v), (lyi.at[gy], lyi_v), (tzf, tzf_v), (tzi, tzi_v),
             (tx, tx_v), (e1, e1_v), (e2, e2_v), (ecol, ecol_v), (eh, eh_v), (mask, mask_v), (mh, mh_v), (eye, eye_v)]
    copies = [pltpu.make_async_copy(src, dst, ld.at[n]) for n, (src, dst) in enumerate(loads)]
    for n in (0, 5):
        copies[n].start()

    xs4 = [(x + dx) % 4 for dx in FAR_X]
    peers = []
    for dz in FAR_Z:
        zz = (z + dz) % 8
        base, hi2 = (zz % 4) * 4, (zz // 4) * 2
        for n, dx in enumerate(FAR_X):
            for dc in (1, 0):
                if dz or dx or dc:
                    peers.append((base + xs4[n], hi2 + (s + dc) % 2))

    barrier = pltpu.get_barrier_semaphore()

    def greet(px, py):
        pl.semaphore_signal(barrier, inc=1, device_id=(px, py), device_id_type=MESH)

    for px in (gxm, gx, gxp):
        for py in (gym, gyp):
            greet(px, py)
    for px, pj in peers:
        greet(px, 4 * y + pj)
    for step in (2, 1, 3):
        greet(gx, (gy + 4 * step) % 16)
    for n in (3, 1, 14, 2, 10, 11, 12, 13, 7, 8, 9, 4, 6):
        copies[n].start()

    copies[0].wait()
    for yy in range(16):
        a = jnp.concatenate([fv[pl.ds(c * 128 + yy, 8, stride=16), :] for c in range(16)], 0)
        hi, lo = hilo(a)
        lanes = slice((yy + 1) * 128, (yy + 2) * 128)
        b[0:128, lanes] = hi
        b[128:256, lanes] = lo
        b[256:384, lanes] = hi
        if yy in (0, 15):
            yh_s[0 if yy == 0 else 1] = a

    copies[5].wait()

    def along_z(h):
        r0 = pl.multiple_of(h * 64, 64)
        for yy in range(8):
            l0 = (2 * yy + 1) * 128
            hi = jnp.concatenate([b[pl.ds(r0, 64), l0:l0 + 128], b[pl.ds(r0, 64), l0 + 128:l0 + 256]], 0)
            lo = jnp.concatenate([b[pl.ds(r0 + 128, 64), l0:l0 + 128], b[pl.ds(r0 + 128, 64), l0 + 128:l0 + 256]], 0)
            r = mm(tzf_v[...], jnp.concatenate([hi, hi, lo], 1), (((1,), (1,)), ((), ())))
            za[h, pl.ds(yy, 24, stride=8), :] = r

    along_z(1 - s)
    pl.semaphore_wait(barrier, 72)

    def remote(src, dst, ssem, rsem, px, py):
        return pltpu.make_async_remote_copy(src_ref=src, dst_ref=dst, send_sem=ssem, recv_sem=rsem,
                                            device_id=(px, py), device_id_type=MESH)

    partner = jj + 1 - 2 * s + 4 * y
    acopies = [remote(za.at[1 - s, pl.ds(48 * n, 48)], zr.at[pl.ds(48 * n, 48)], a_s.at[n], a_r.at[n], gx, partner)
               for n in range(4)]
    for copy in acopies:
        copy.start()
    halos = [
        remote(f3.at[:, pl.ds(112, 16), :], xh.at[0], h_s.at[0], h_r.at[0], gxp, gy),
        remote(f3.at[:, pl.ds(0, 16), :], xh.at[1], h_s.at[1], h_r.at[1], gxm, gy),
    ]
    for copy in halos:
        copy.start()
    along_z(s)

    copies[1].wait()
    copies[14].wait()
    for n in range(4):
        t = lax.dot_general(eye_v[...], wv[pl.ds(128 * n, 128), :], (((1,), (1,)), ((), ())),
                            precision=lax.Precision.HIGHEST, preferred_element_type=F32)
        for m in range(27):
            ws[m, n, :] = t[m, :]

    copies[3].wait()
    half = lax.broadcasted_iota(jnp.int32, (24, 128), 1) < 64
    for k in range(12):
        if k % 3 == 0:
            acopies[k // 3].wait_recv()
        v = jnp.concatenate([za[s, 16 * k:16 * k + 16, :], zr[16 * k:16 * k + 16, :]], 0)
        hi, lo = hilo(v)
        r = mm(lyf_v[...], jnp.concatenate([hi, hi, lo], 0))
        p0 = jnp.where(half, r[0:24], r[72:96])
        p1 = jnp.where(half, r[24:48], r[48:72])
        ps[pl.ds(k, 24, stride=12), :] = p0 + pltpu.roll(p1, 64, 1)

    ycopies = []
    for step in (2, 1, 3):
        yt = (y + step) % 4
        copy = remote(ps.at[pl.ds(pl.multiple_of(yt * 72, 8), 72), :], pr.at[step - 1], y_s.at[step - 1],
                      y_r.at[step - 1], gx, yt * 4 + jj)
        copy.start()
        ycopies.append(copy)

    def w_copy(m):
        mode = 27 * gx + m
        r = 18 * jj + mode % 18
        d = 8 * (r // 9) + jnp.maximum(r % 9 - 1, 0)
        slot = (r % 9 == 1).astype(jnp.int32)
        p = mode // 18
        return d, slot, p, remote(ws.at[m], wb.at[slot, p], w_s.at[m], w_r.at[slot], d // 4, y * 4 + d % 4)

    def w_send(m, carry):
        d, slot, p, copy = w_copy(m)

        @pl.when(d != me)
        def _():
            copy.start()

        @pl.when(d == me)
        def _():
            pltpu.make_async_copy(ws.at[m], wb.at[slot, p], w_r.at[slot]).start()
        return carry

    lax.fori_loop(0, 27, w_send, 0)

    for n, (x0, y0) in enumerate(((0, 0), (0, 15), (7, 0), (7, 15))):
        cs[n] = jnp.concatenate([fv[pl.ds(c * 128 + x0 * 16 + y0, 1), :] for c in range(16)], 0)
    more = [
        remote(yh_s.at[1], yh.at[0], h_s.at[2], h_r.at[2], gx, gyp),
        remote(yh_s.at[0], yh.at[1], h_s.at[3], h_r.at[3], gx, gym),
        remote(cs.at[0], ch.at[3], h_s.at[4], h_r.at[7], gxm, gym),
        remote(cs.at[1], ch.at[2], h_s.at[5], h_r.at[6], gxm, gyp),
        remote(cs.at[2], ch.at[1], h_s.at[6], h_r.at[5], gxp, gym),
        remote(cs.at[3], ch.at[0], h_s.at[7], h_r.at[4], gxp, gyp),
    ]
    for copy in more:
        copy.start()
    halos = halos + more
    rs[72] = jnp.zeros((1, 128), F32)

    for copy in ycopies:
        copy.wait_recv()
    total = ps[pl.ds(pl.multiple_of(y * 72, 8), 72), :] + pr[0] + pr[1] + pr[2]
    for r in range(72):
        rs[r, :, :] = total[r:r + 1, :]

    def b_copy(px, pj):
        d = px * 4 + pj
        u8 = d % 8
        r = 9 * (d // 8) + u8 + (u8 > 0).astype(jnp.int32)
        return rs.at[pl.ds(r, 2)], px, 4 * y + pj

    for px, pj in peers:
        src, dx, dy = b_copy(px, pj)
        remote(src, rb.at[me], b_s, b_r, dx, dy).start()
    src, _, _ = b_copy(gx, jj)
    pltpu.make_async_copy(src, rb.at[me], b_r).start()
    double = me % 8 == 0

    for n in (2, 10, 11, 12, 13):
        copies[n].wait()
    cwt = lax.dot_general(eye_v[...], cwv[...], (((1,), (1,)), ((), ())),
                          precision=lax.Precision.HIGHEST, preferred_element_type=F32)
    group = lax.broadcasted_iota(jnp.int32, (32, 256), 1) // 16
    picked = jnp.concatenate([jnp.where(group == o, cwt, 0.0) for o in range(16)], 0)
    whi, wlo = hilo(picked)
    xs[0] = mm(whi, ecol_v[...])
    xs[1] = mm(wlo, ecol_v[...])
    xs[2] = mm(whi, eh_v[0]) + mm(wlo, eh_v[1])

    def spread(op, carry):
        for t in range(3):
            ms = [mask_v[a] > 0 if t < 2 else mh_v[a] > 0 for a in range(3)]
            for yb in range(3):
                parts = []
                for oo in range(2):
                    for zc in range(3):
                        v = jnp.zeros((8, 128), F32)
                        for a in range(3) if t < 2 else (0, 2):
                            row = xs[t, pl.ds((2 * op + oo) * 32 + 9 * a + 3 * yb + zc, 1), :]
                            v = jnp.where(ms[a], jnp.broadcast_to(row, (8, 128)), v)
                        parts.append(v)
                v = jnp.concatenate(parts, 0).astype(BF16)
                rows = pl.ds(pl.multiple_of(384 * yb + 48 * op, 16), 48)
                if t == 0:
                    lhs[rows, 0:128] = v
                    lhs[rows, 128:256] = v
                else:
                    lhs[rows, 128 + 128 * t:256 + 128 * t] = v
        return carry

    lax.fori_loop(0, 8, spread, 0)

    b[384:512, :] = jnp.zeros((128, 18 * 128), BF16)
    for copy in halos:
        copy.wait_recv()
    for yi, side in ((0, 0), (17, 1)):
        hi, lo = hilo(yh[side])
        lanes = slice(yi * 128, yi * 128 + 128)
        b[0:128, lanes] = hi
        b[128:256, lanes] = lo
        b[256:384, lanes] = hi
    for yi in range(18):
        if yi == 0:
            v = jnp.concatenate([ch[0], ch[2]], 0)
        elif yi == 17:
            v = jnp.concatenate([ch[1], ch[3]], 0)
        else:
            v = jnp.concatenate([xh[side, c, pl.ds(yi - 1, 1), :] for side in range(2) for c in range(16)], 0)
        hi, lo = hilo(v)
        b[384:480, yi * 128:yi * 128 + 128] = jnp.concatenate([hi, hi, lo], 0)

    def conv(pair, carry):
        acc = jnp.zeros((384, 256), F32)
        for t in range(3):
            lanes = pl.ds(pl.multiple_of((2 * pair + t) * 128, 128), 256)
            acc = acc + mm(lhs[384 * t:384 * t + 384, :], b[:, lanes])
        for n in range(2):
            v = acc[:, 128 * n:128 * n + 128].reshape(16, 3, 8, 128)
            v0, v1, v2 = (v[:, i].reshape(128, 128) for i in range(3))
            v = v1 + pltpu.roll(v0, 1, 1) + pltpu.roll(v2, 127, 1)
            v_out[pl.ds(pl.multiple_of((2 * pair + n) * 128, 128), 128), :] = v
        return carry

    for n in (7, 8, 9):
        copies[n].wait()
    pltpu.make_async_copy(wb.at[0], wb.at[0], w_r.at[0]).wait()

    @pl.when(double)
    def _():
        pltpu.make_async_copy(wb.at[1], wb.at[1], w_r.at[1]).wait()

    pltpu.make_async_copy(rb, rb, b_r).wait()

    def mix(slots):
        accs = [[[jnp.zeros((24, 128), F32) for _ in range(2)] for _ in range(2)] for _ in slots]
        for g in range(16):
            for core in range(2):
                for n, slot in enumerate(slots):
                    row = rb[4 * g + core, slot] + rb[4 * g + core + 2, slot]
                    row = jnp.broadcast_to(row, (24, 128))
                    for part in range(2):
                        accs[n][part][core] = accs[n][part][core] + tx_v[part, g] * row
        acc = jnp.concatenate([jnp.concatenate(accs[n][part], 1) for n in range(len(slots)) for part in range(2)], 0)
        size = 48 * len(slots)
        hi, lo = hilo(acc)
        cc = mm(jnp.concatenate([hi, lo], 0), e1_v[...])
        cc = cc[0:size] + cc[size:2 * size]
        prods = []
        for n, slot in enumerate(slots):
            cr, ci = cc[48 * n:48 * n + 24], cc[48 * n + 24:48 * n + 48]
            w4 = [jnp.concatenate([wb[slot, p, pl.ds(t, 1), :] for p in range(24)], 0) for t in range(4)]
            wr = jnp.concatenate(w4[0:2], 1)
            wi = jnp.concatenate(w4[2:4], 1)
            prods += [wr * cr - wi * ci, wr * ci + wi * cr]
        hi, lo = hilo(jnp.concatenate(prods, 0))
        mx = mm(jnp.concatenate([hi, lo], 0), e2_v[...])
        mx = mx[0:size] + mx[size:2 * size]
        for g in range(16):
            for core in range(2):
                for n, slot in enumerate(slots):
                    lanes = slice(128 * core, 128 * core + 128)
                    row = tx_v[0, g] * mx[48 * n:48 * n + 24, lanes] + tx_v[1, g] * mx[48 * n + 24:48 * n + 48, lanes]
                    co_s[2 * g + core, slot] = jnp.sum(row, axis=0, keepdims=True)
                if len(slots) == 1:
                    co_s[2 * g + core, 1] = jnp.zeros((1, 128), F32)

    @pl.when(double)
    def _():
        mix((0, 1))

    @pl.when(jnp.logical_not(double))
    def _():
        mix((0,))

    for px, pj in peers:
        remote(co_s.at[2 * px + pj % 2], rc.at[me], c_s, c_r, px, 4 * y + pj).start()
    pltpu.make_async_copy(co_s.at[2 * gx + s], rc.at[me], c_r).start()

    lax.fori_loop(0, 8, conv, 0)

    for t in range(4):
        g3[t, 72:96, :] = jnp.zeros((24, 128), F32)
    pltpu.make_async_copy(rc, rc, c_r).wait()
    for r in range(72):
        t8, u8 = r // 9, r % 9
        g3[0, r:r + 1, :] = rc[8 * t8 + max(u8 - 1, 0), 1 if u8 == 1 else 0]
    dcopies = []
    for step in (2, 1, 3):
        yt = (y + step) % 4
        copy = remote(g3.at[0, pl.ds(0, 72)], g3.at[4 - step, pl.ds(0, 72)], d_s.at[step - 1], d_r.at[4 - step],
                      gx, yt * 4 + jj)
        copy.start()
        dcopies.append(copy)
    copies[4].wait()
    copies[6].wait()
    for copy in dcopies:
        copy.wait_recv()

    half16 = lax.broadcasted_iota(jnp.int32, (16, 128), 1) < 64
    for k in range(12):
        v = jnp.concatenate([g3[(t - y + 4) % 4, pl.ds(k, 8, stride=12), :] for t in range(4)], 0)
        v = jnp.concatenate([v, pltpu.roll(v, 64, 1)], 0)
        hi, lo = hilo(v)
        r = mm(lyi_v[...], jnp.concatenate([hi, hi, lo], 0))
        for part in range(2):
            v = jnp.where(half16, r[16 * part:16 * part + 16], r[32 + 16 * part:48 + 16 * part])
            for dst in range(2):
                u[dst, pl.ds(2 * k + part, 8, stride=24), :] = v[8 * dst:8 * dst + 8]

    ucopies = [remote(u.at[1, pl.ds(48 * n, 48)], ur.at[pl.ds(48 * n, 48)], u_s.at[n], u_r.at[n], gx, partner)
               for n in range(4)]
    for copy in ucopies:
        copy.start()

    zero8 = jnp.zeros((8, 128), F32)

    def finish(v, hh, yy):
        hi, lo = hilo(jnp.concatenate([v, zero8], 0))
        r = mm(jnp.concatenate([hi, hi, lo], 0), tzi_v[...], (((0,), (0,)), ((), ())))
        for yp in range(2):
            rows = pl.ds(pl.multiple_of((2 * yy + yp) * 128 + hh * 64, 64), 64)
            v_out[rows, :] = v_out[rows, :] + r[64 * yp:64 * yp + 64]

    for yy in range(8):
        finish(u[0, 24 * yy:24 * yy + 24, :], s, yy)
    for yy in range(8):
        if yy % 2 == 0:
            ucopies[yy // 2].wait_recv()
        finish(ur[24 * yy:24 * yy + 24, :], 1 - s, yy)

    for copy in acopies + ucopies + halos + ycopies + dcopies:
        copy.wait_send()

    def w_done(m, carry):
        d, slot, p, copy = w_copy(m)

        @pl.when(d != me)
        def _():
            copy.wait_send()
        return carry

    lax.fori_loop(0, 27, w_done, 0)
    part = rb.at[pl.ds(0, 63)]
    pltpu.make_async_copy(part, part, b_s).wait()
    pltpu.make_async_copy(part, part, c_s).wait()


def gelu_kernel(v, out_hbm, outv, sem):
    copies = []
    for n in range(4):
        for yr in range(16):
            t = gelu(v[yr * 128 + 32 * n:yr * 128 + 32 * n + 32, :])
            for c in range(4):
                outv[pl.ds((4 * n + c) * 128 + yr, 8, stride=16), :] = t[8 * c:8 * c + 8]
        rows = pl.ds(512 * n, 512)
        copy = pltpu.make_async_copy(outv.at[rows], out_hbm.at[rows], sem.at[n])
        copy.start()
        copies.append(copy)
    for copy in copies:
        copy.wait()


def shards(features, conv_weight, mix_weight):
    f2 = features.reshape(2048, 128)
    f3 = features.reshape(16, 128, 128)
    w = mix_weight.reshape(512, 27)
    cw = conv_weight.transpose(1, 2, 0).reshape(256, 27)
    consts = [jnp.asarray(TABLES[n]) for n in NAMES]
    vm = pltpu.VMEM
    dma = pltpu.SemaphoreType.DMA
    scratch = [
        vm((2048, 128), F32), vm((512, 27), F32), vm((256, 27), F32),
        vm((24, 384), BF16), vm((96, 128), BF16), vm((2, 16, 24, 128), F32), vm((256, 256), BF16), vm((256, 256), BF16),
        vm((256, 128), BF16), vm((2, 256, 128), BF16), vm((3, 8, 128), F32), vm((3, 8, 128), F32), vm((32, 27), F32),
        vm((96, 96), BF16), vm((64, 192), BF16),
        vm((27, 4, 128), F32), vm((2, 24, 4, 128), F32), vm((512, 18 * 128), BF16), vm((1152, 512), BF16),
        vm((3, 512, 128), F32),
        vm((2, 128, 128), F32), vm((2, 128, 128), F32), vm((2, 16, 16, 128), F32), vm((4, 16, 128), F32),
        vm((4, 16, 128), F32), vm((2, 192, 128), F32), vm((192, 128), F32), vm((288, 128), F32), vm((3, 72, 128), F32),
        vm((73, 1, 128), F32), vm((64, 2, 1, 128), F32), vm((32, 2, 1, 128), F32), vm((64, 2, 1, 128), F32),
        vm((4, 96, 128), F32), vm((2, 192, 128), F32), vm((192, 128), F32),
        dma((15,)), dma((4,)), dma((4,)), dma((8,)), dma((8,)), dma((3,)), dma((3,)), dma, dma, dma, dma,
        dma((3,)), dma((4,)), dma((27,)), dma((2,)), dma((4,)), dma((4,)),
    ]
    any_spec = pl.BlockSpec(memory_space=pl.ANY)
    vmem_spec = pl.BlockSpec(memory_space=pltpu.VMEM)
    hbm_spec = pl.BlockSpec(memory_space=pltpu.HBM)
    v = pl.pallas_call(
        kernel,
        out_shape=jax.ShapeDtypeStruct((2048, 128), F32),
        in_specs=[hbm_spec] * (4 + len(NAMES)),
        out_specs=vmem_spec,
        scratch_shapes=scratch,
        compiler_params=pltpu.CompilerParams(collective_id=0, has_side_effects=True,
                                             vmem_limit_bytes=40 * 1024 * 1024),
        name="layer",
    )(*[pltpu.with_memory_space_constraint(a, pltpu.HBM) for a in (f2, f3, w, cw, *consts)])
    out = pl.pallas_call(
        gelu_kernel,
        out_shape=jax.ShapeDtypeStruct((2048, 128), F32),
        in_specs=[vmem_spec],
        out_specs=any_spec,
        scratch_shapes=[vm((2048, 128), F32), dma((4,))],
        compiler_params=pltpu.CompilerParams(vmem_limit_bytes=8 * 1024 * 1024),
        name="act",
    )(v)
    return out.reshape(features.shape)


def solution(mesh):
    in_specs = (P(None, "gx", "gy", None), P(), P(None, None, None, "gy", "gx"))
    return jax.shard_map(shards, mesh=mesh, in_specs=in_specs, out_specs=P(None, "gx", "gy", None), check_vma=False)
```

time: 47.2 us -> 42.4 us (0.90)
  local copies, waits for them, and re-layouts: 4.06 us -> 0 us
  Pallas kernels: 43 us -> 42.3 us
    unnamed x2 -> x0, local copies, waits for them, and re-layouts: 4.06 us -> none
    pallas_call x1, Pallas kernels: 43 us -> 40.4 us  [shards(): pl.pallas_call(kernel, out_shape=jax.ShapeDtypeStruct((2048, 128), F32),...]
    pallas_call x0 -> x1, Pallas kernels: none -> 1.88 us  [shards(): pl.pallas_call(gelu_kernel, out_shape=jax.ShapeDtypeStruct((2048, 128), F...]
where the time goes in v2:
time: 42.4 us; the launch traced here: 42.3 us
  Pallas kernels  42.3 us (100%)
    pallas_call x1, Pallas kernels, shards(): pl.pallas_call(kernel, out_shape=jax.ShapeDtypeStruct((2048, 128), F32),...  40.4 us
    pallas_call x1, Pallas kernels, shards(): pl.pallas_call(gelu_kernel, out_shape=jax.ShapeDtypeStruct((2048, 128), F...  1.88 us

profile of v2, /device:TPU:1, one launch (start us, length us, event | category | flops | bytes accessed | tf_op | source)
XLA Modules:
  0.0 42.3 jit_solution(5824377670184678610)
XLA Ops:
  0.0 40.4 %layer.1.v = f32[2048,128]{1,0:T(8,128)S(1)} custom-call(f32[2048,128]{1,0:T(8,128)} %bitcast.7, f32[16,128,128]{2,1,0:T(8,128)} %bitcast.8, f32[512,27]{1,0:T(8,128)} %bitcast.9, f32[256,27]{1,0:T(8,128)} %bitcast.10, bf16[24,384]{1,0:T(8,128)(2,1)} %constant.24.clone.tzf, bf16[96,128]{1,0:T(8,128)(2,1)} %constant.25.clone.tzi, ...), custom_call_target="tpu_custom_call" | custom-call | tf_op jit(solution)/shard_map/layer/pallas_call | solution.py:544
  40.4 1.9 %act.1 = f32[2048,128]{1,0:T(8,128)} custom-call(f32[2048,128]{1,0:T(8,128)S(1)} %layer.1.v), custom_call_target="tpu_custom_call" | custom-call | tf_op jit(solution)/shard_map/act/pallas_call | solution.py:554

commit v3 on v2

--- a/solution.py
+++ b/solution.py
@@ -142,7 +142,7 @@
 
 def kernel(f2, f3, w_hbm, cw, tzf, tzi, lyf, lyi, tx, e1, e2, ecol, eh, mask, mh, eye, v_out, *refs):
     (fv, wv, cwv, tzf_v, tzi_v, tx_v, e1_v, e2_v, ecol_v, eh_v, mask_v, mh_v, eye_v, lyf_v, lyi_v,
-     ws, wb, b, lhs, xs, yh_s, yh, xh, cs, ch, za, zr, ps, pr, rs, rb, co_s, rc, g3, u, ur,
+     ws, wb, wg, b, lhs, xs, yh_s, yh, xh, cs, ch, za, zr, ps, pr, rs, rb, co_s, rc, g3, u, ur, co,
      ld, a_s, a_r, h_s, h_r, y_s, y_r, b_s, b_r, c_s, c_r, d_s, d_r, w_s, w_r, u_s, u_r) = refs
     gx = lax.axis_index("gx")
     gy = lax.axis_index("gy")
@@ -151,14 +151,17 @@
     s = gy % 2
     x = gx % 4
     z = (gx // 4) + 4 * (jj // 2)
-    me = gx * 4 + jj
+    me = jj * 16 + gx
     gxm, gxp = (gx + 15) % 16, (gx + 1) % 16
     gym, gyp = (gy + 15) % 16, (gy + 1) % 16
 
-    loads = [(f2, fv), (w_hbm, wv), (cw, cwv), (lyf.at[gy], lyf_v), (lyi.at[gy], lyi_v), (tzf, tzf_v), (tzi, tzi_v),
-             (tx, tx_v), (e1, e1_v), (e2, e2_v), (ecol, ecol_v), (eh, eh_v), (mask, mask_v), (mh, mh_v), (eye, eye_v)]
+    far = pl.multiple_of((1 - s) * 1024, 1024)
+    near = pl.multiple_of(s * 1024, 1024)
+    loads = [(f2.at[pl.ds(far, 1024)], fv.at[pl.ds(far, 1024)]), (w_hbm, wv), (cw, cwv), (lyf.at[gy], lyf_v), (lyi.at[gy], lyi_v), (tzf, tzf_v), (tzi, tzi_v),
+             (tx, tx_v), (e1, e1_v), (e2, e2_v), (ecol, ecol_v), (eh, eh_v), (mask, mask_v), (mh, mh_v), (eye, eye_v),
+             (f2.at[pl.ds(near, 1024)], fv.at[pl.ds(near, 1024)])]
     copies = [pltpu.make_async_copy(src, dst, ld.at[n]) for n, (src, dst) in enumerate(loads)]
-    for n in (0, 5):
+    for n in (0, 5, 15):
         copies[n].start()
 
     xs4 = [(x + dx) % 4 for dx in FAR_X]
@@ -171,6 +174,7 @@
                 if dz or dx or dc:
                     peers.append((base + xs4[n], hi2 + (s + dc) % 2))
 
+    partner = jj + 1 - 2 * s + 4 * y
     barrier = pltpu.get_barrier_semaphore()
 
     def greet(px, py):
@@ -186,18 +190,17 @@
     for n in (3, 1, 14, 2, 10, 11, 12, 13, 7, 8, 9, 4, 6):
         copies[n].start()
 
-    copies[0].wait()
-    for yy in range(16):
-        a = jnp.concatenate([fv[pl.ds(c * 128 + yy, 8, stride=16), :] for c in range(16)], 0)
-        hi, lo = hilo(a)
-        lanes = slice((yy + 1) * 128, (yy + 2) * 128)
-        b[0:128, lanes] = hi
-        b[128:256, lanes] = lo
-        b[256:384, lanes] = hi
-        if yy in (0, 15):
-            yh_s[0 if yy == 0 else 1] = a
-
-    copies[5].wait()
+    def part(h):
+        r0 = pl.multiple_of(h * 64, 64)
+        for yy in range(16):
+            a = jnp.concatenate([fv[pl.ds(h * 1024 + c * 128 + yy, 8, stride=16), :] for c in range(8)], 0)
+            hi, lo = hilo(a)
+            lanes = slice((yy + 1) * 128, (yy + 2) * 128)
+            b[pl.ds(r0, 64), lanes] = hi
+            b[pl.ds(r0 + 128, 64), lanes] = lo
+            b[pl.ds(r0 + 256, 64), lanes] = hi
+            if yy in (0, 15):
+                yh_s[0 if yy == 0 else 1, pl.ds(r0, 64), :] = a
 
     def along_z(h):
         r0 = pl.multiple_of(h * 64, 64)
@@ -208,6 +211,9 @@
             r = mm(tzf_v[...], jnp.concatenate([hi, hi, lo], 1), (((1,), (1,)), ((), ())))
             za[h, pl.ds(yy, 24, stride=8), :] = r
 
+    copies[0].wait()
+    part(1 - s)
+    copies[5].wait()
     along_z(1 - s)
     pl.semaphore_wait(barrier, 72)
 
@@ -215,7 +221,6 @@
         return pltpu.make_async_remote_copy(src_ref=src, dst_ref=dst, send_sem=ssem, recv_sem=rsem,
                                             device_id=(px, py), device_id_type=MESH)
 
-    partner = jj + 1 - 2 * s + 4 * y
     acopies = [remote(za.at[1 - s, pl.ds(48 * n, 48)], zr.at[pl.ds(48 * n, 48)], a_s.at[n], a_r.at[n], gx, partner)
                for n in range(4)]
     for copy in acopies:
@@ -223,9 +228,26 @@
     halos = [
         remote(f3.at[:, pl.ds(112, 16), :], xh.at[0], h_s.at[0], h_r.at[0], gxp, gy),
         remote(f3.at[:, pl.ds(0, 16), :], xh.at[1], h_s.at[1], h_r.at[1], gxm, gy),
+        remote(yh_s.at[1], yh.at[0], h_s.at[2], h_r.at[2], gx, gyp),
+        remote(yh_s.at[0], yh.at[1], h_s.at[3], h_r.at[3], gx, gym),
+        remote(cs.at[0], ch.at[3], h_s.at[4], h_r.at[7], gxm, gym),
+        remote(cs.at[1], ch.at[2], h_s.at[5], h_r.at[6], gxm, gyp),
+        remote(cs.at[2], ch.at[1], h_s.at[6], h_r.at[5], gxp, gym),
+        remote(cs.at[3], ch.at[0], h_s.at[7], h_r.at[4], gxp, gyp),
     ]
-    for copy in halos:
+    for copy in halos[0:2]:
         copy.start()
+    copies[15].wait()
+    part(s)
+
+    @pl.when(jj != 3)
+    def _():
+        halos[2].start()
+
+    @pl.when(jj != 0)
+    def _():
+        halos[3].start()
+
     along_z(s)
 
     copies[1].wait()
@@ -235,6 +257,29 @@
                             precision=lax.Precision.HIGHEST, preferred_element_type=F32)
         for m in range(27):
             ws[m, n, :] = t[m, :]
+
+    odd = gx % 2 == 1
+
+    def w_copy(m):
+        picks = []
+        for mode in (m, m + 27):
+            l = mode % 18
+            d = 8 * (l // 9) + max(l % 9 - 1, 0)
+            picks.append((d, int(l % 9 == 1), mode // 18))
+        dx, slot, p = (a if a == b else jnp.where(odd, b, a) for a, b in zip(*picks))
+        p = 3 * (gx // 2) + p
+        mine = dx == gx
+        return mine, slot, p, remote(ws.at[m], wb.at[slot, p], w_s.at[m], w_r.at[slot], dx, gy)
+
+    wcopies = [w_copy(m) for m in range(27)]
+    for m, (mine, slot, p, copy) in enumerate(wcopies):
+        @pl.when(jnp.logical_not(mine))
+        def _():
+            copy.start()
+
+        @pl.when(mine)
+        def _():
+            pltpu.make_async_copy(ws.at[m], wb.at[slot, p], w_r.at[slot]).start()
 
     copies[3].wait()
     half = lax.broadcasted_iota(jnp.int32, (24, 128), 1) < 64
@@ -256,42 +301,20 @@
         copy.start()
         ycopies.append(copy)
 
-    def w_copy(m):
-        mode = 27 * gx + m
-        r = 18 * jj + mode % 18
-        d = 8 * (r // 9) + jnp.maximum(r % 9 - 1, 0)
-        slot = (r % 9 == 1).astype(jnp.int32)
-        p = mode // 18
-        return d, slot, p, remote(ws.at[m], wb.at[slot, p], w_s.at[m], w_r.at[slot], d // 4, y * 4 + d % 4)
-
-    def w_send(m, carry):
-        d, slot, p, copy = w_copy(m)
-
-        @pl.when(d != me)
-        def _():
-            copy.start()
-
-        @pl.when(d == me)
-        def _():
-            pltpu.make_async_copy(ws.at[m], wb.at[slot, p], w_r.at[slot]).start()
-        return carry
-
-    lax.fori_loop(0, 27, w_send, 0)
+    @pl.when(jj == 3)
+    def _():
+        halos[2].start()
+
+    @pl.when(jj == 0)
+    def _():
+        halos[3].start()
 
     for n, (x0, y0) in enumerate(((0, 0), (0, 15), (7, 0), (7, 15))):
         cs[n] = jnp.concatenate([fv[pl.ds(c * 128 + x0 * 16 + y0, 1), :] for c in range(16)], 0)
-    more = [
-        remote(yh_s.at[1], yh.at[0], h_s.at[2], h_r.at[2], gx, gyp),
-        remote(yh_s.at[0], yh.at[1], h_s.at[3], h_r.at[3], gx, gym),
-        remote(cs.at[0], ch.at[3], h_s.at[4], h_r.at[7], gxm, gym),
-        remote(cs.at[1], ch.at[2], h_s.at[5], h_r.at[6], gxm, gyp),
-        remote(cs.at[2], ch.at[1], h_s.at[6], h_r.at[5], gxp, gym),
-        remote(cs.at[3], ch.at[0], h_s.at[7], h_r.at[4], gxp, gyp),
-    ]
-    for copy in more:
+    rs[72] = jnp.zeros((1, 128), F32)
+    for copy in halos[4:]:
         copy.start()
-    halos = halos + more
-    rs[72] = jnp.zeros((1, 128), F32)
+
 
     for copy in ycopies:
         copy.wait_recv()
@@ -300,7 +323,7 @@
         rs[r, :, :] = total[r:r + 1, :]
 
     def b_copy(px, pj):
-        d = px * 4 + pj
+        d = pj * 16 + px
         u8 = d % 8
         r = 9 * (d // 8) + u8 + (u8 > 0).astype(jnp.int32)
         return rs.at[pl.ds(r, 2)], px, 4 * y + pj
@@ -346,6 +369,77 @@
 
     lax.fori_loop(0, 8, spread, 0)
 
+    def conv(pair, carry):
+        acc = jnp.zeros((384, 256), F32)
+        for t in range(3):
+            lanes = pl.ds(pl.multiple_of((2 * pair + t) * 128, 128), 256)
+            acc = acc + mm(lhs[384 * t:384 * t + 384, :], b[:, lanes])
+        for n in range(2):
+            v = acc[:, 128 * n:128 * n + 128].reshape(16, 3, 8, 128)
+            v0, v1, v2 = (v[:, i].reshape(128, 128) for i in range(3))
+            v = v1 + pltpu.roll(v0, 1, 1) + pltpu.roll(v2, 127, 1)
+            co[pl.ds(pl.multiple_of((2 * pair + n) * 128, 128), 128), :] = v
+        return carry
+
+    for n in (7, 8, 9):
+        copies[n].wait()
+    def gather(slot):
+        pltpu.make_async_copy(wb.at[slot], wb.at[slot], w_r.at[slot]).wait()
+        for t in range(4):
+            for p in range(24):
+                wg[slot, t // 2, p:p + 1, 128 * (t % 2):128 * (t % 2) + 128] = wb[slot, p, t:t + 1, :]
+
+    gather(0)
+
+    @pl.when(double)
+    def _():
+        gather(1)
+
+    pltpu.make_async_copy(rb, rb, b_r).wait()
+
+    def mix(slots):
+        accs = [[[jnp.zeros((24, 128), F32) for _ in range(2)] for _ in range(2)] for _ in slots]
+        for g in range(16):
+            for core in range(2):
+                for n, slot in enumerate(slots):
+                    row = rb[16 * core + g, slot] + rb[16 * core + 32 + g, slot]
+                    row = jnp.broadcast_to(row, (24, 128))
+                    for part in range(2):
+                        accs[n][part][core] = accs[n][part][core] + tx_v[part, g] * row
+        acc = jnp.concatenate([jnp.concatenate(accs[n][part], 1) for n in range(len(slots)) for part in range(2)], 0)
+        size = 48 * len(slots)
+        hi, lo = hilo(acc)
+        cc = mm(jnp.concatenate([hi, lo], 0), e1_v[...])
+        cc = cc[0:size] + cc[size:2 * size]
+        prods = []
+        for n, slot in enumerate(slots):
+            cr, ci = cc[48 * n:48 * n + 24], cc[48 * n + 24:48 * n + 48]
+            wr, wi = wg[slot, 0], wg[slot, 1]
+            prods += [wr * cr - wi * ci, wr * ci + wi * cr]
+        hi, lo = hilo(jnp.concatenate(prods, 0))
+        mx = mm(jnp.concatenate([hi, lo], 0), e2_v[...])
+        mx = mx[0:size] + mx[size:2 * size]
+        for g in range(16):
+            for core in range(2):
+                for n, slot in enumerate(slots):
+                    lanes = slice(128 * core, 128 * core + 128)
+                    row = tx_v[0, g] * mx[48 * n:48 * n + 24, lanes] + tx_v[1, g] * mx[48 * n + 24:48 * n + 48, lanes]
+                    co_s[2 * g + core, slot] = jnp.sum(row, axis=0, keepdims=True)
+                if len(slots) == 1:
+                    co_s[2 * g + core, 1] = jnp.zeros((1, 128), F32)
+
+    @pl.when(double)
+    def _():
+        mix((0, 1))
+
+    @pl.when(jnp.logical_not(double))
+    def _():
+        mix((0,))
+
+    for px, pj in peers:
+        remote(co_s.at[2 * px + pj % 2], rc.at[me], c_s, c_r, px, 4 * y + pj).start()
+    pltpu.make_async_copy(co_s.at[2 * gx + s], rc.at[me], c_r).start()
+
     b[384:512, :] = jnp.zeros((128, 18 * 128), BF16)
     for copy in halos:
         copy.wait_recv()
@@ -365,73 +459,6 @@
         hi, lo = hilo(v)
         b[384:480, yi * 128:yi * 128 + 128] = jnp.concatenate([hi, hi, lo], 0)
 
-    def conv(pair, carry):
-        acc = jnp.zeros((384, 256), F32)
-        for t in range(3):
-            lanes = pl.ds(pl.multiple_of((2 * pair + t) * 128, 128), 256)
-            acc = acc + mm(lhs[384 * t:384 * t + 384, :], b[:, lanes])
-        for n in range(2):
-            v = acc[:, 128 * n:128 * n + 128].reshape(16, 3, 8, 128)
-            v0, v1, v2 = (v[:, i].reshape(128, 128) for i in range(3))
-            v = v1 + pltpu.roll(v0, 1, 1) + pltpu.roll(v2, 127, 1)
-            v_out[pl.ds(pl.multiple_of((2 * pair + n) * 128, 128), 128), :] = v
-        return carry
-
-    for n in (7, 8, 9):
-        copies[n].wait()
-    pltpu.make_async_copy(wb.at[0], wb.at[0], w_r.at[0]).wait()
-
-    @pl.when(double)
-    def _():
-        pltpu.make_async_copy(wb.at[1], wb.at[1], w_r.at[1]).wait()
-
-    pltpu.make_async_copy(rb, rb, b_r).wait()
-
-    def mix(slots):
-        accs = [[[jnp.zeros((24, 128), F32) for _ in range(2)] for _ in range(2)] for _ in slots]
-        for g in range(16):
-            for core in range(2):
-                for n, slot in enumerate(slots):
-                    row = rb[4 * g + core, slot] + rb[4 * g + core + 2, slot]
-                    row = jnp.broadcast_to(row, (24, 128))
-                    for part in range(2):
-                        accs[n][part][core] = accs[n][part][core] + tx_v[part, g] * row
-        acc = jnp.concatenate([jnp.concatenate(accs[n][part], 1) for n in range(len(slots)) for part in range(2)], 0)
-        size = 48 * len(slots)
-        hi, lo = hilo(acc)
-        cc = mm(jnp.concatenate([hi, lo], 0), e1_v[...])
-        cc = cc[0:size] + cc[size:2 * size]
-        prods = []
-        for n, slot in enumerate(slots):
-            cr, ci = cc[48 * n:48 * n + 24], cc[48 * n + 24:48 * n + 48]
-            w4 = [jnp.concatenate([wb[slot, p, pl.ds(t, 1), :] for p in range(24)], 0) for t in range(4)]
-            wr = jnp.concatenate(w4[0:2], 1)
-            wi = jnp.concatenate(w4[2:4], 1)
-            prods += [wr * cr - wi * ci, wr * ci + wi * cr]
-        hi, lo = hilo(jnp.concatenate(prods, 0))
-        mx = mm(jnp.concatenate([hi, lo], 0), e2_v[...])
-        mx = mx[0:size] + mx[size:2 * size]
-        for g in range(16):
-            for core in range(2):
-                for n, slot in enumerate(slots):
-                    lanes = slice(128 * core, 128 * core + 128)
-                    row = tx_v[0, g] * mx[48 * n:48 * n + 24, lanes] + tx_v[1, g] * mx[48 * n + 24:48 * n + 48, lanes]
-                    co_s[2 * g + core, slot] = jnp.sum(row, axis=0, keepdims=True)
-                if len(slots) == 1:
-                    co_s[2 * g + core, 1] = jnp.zeros((1, 128), F32)
-
-    @pl.when(double)
-    def _():
-        mix((0, 1))
-
-    @pl.when(jnp.logical_not(double))
-    def _():
-        mix((0,))
-
-    for px, pj in peers:
-        remote(co_s.at[2 * px + pj % 2], rc.at[me], c_s, c_r, px, 4 * y + pj).start()
-    pltpu.make_async_copy(co_s.at[2 * gx + s], rc.at[me], c_r).start()
-
     lax.fori_loop(0, 8, conv, 0)
 
     for t in range(4):
@@ -452,6 +479,8 @@
     for copy in dcopies:
         copy.wait_recv()
 
+    ucopies = [remote(u.at[1, pl.ds(48 * n, 48)], ur.at[pl.ds(48 * n, 48)], u_s.at[n], u_r.at[n], gx, partner)
+               for n in range(4)]
     half16 = lax.broadcasted_iota(jnp.int32, (16, 128), 1) < 64
     for k in range(12):
         v = jnp.concatenate([g3[(t - y + 4) % 4, pl.ds(k, 8, stride=12), :] for t in range(4)], 0)
@@ -461,55 +490,52 @@
         for part in range(2):
             v = jnp.where(half16, r[16 * part:16 * part + 16], r[32 + 16 * part:48 + 16 * part])
             for dst in range(2):
-                u[dst, pl.ds(2 * k + part, 8, stride=24), :] = v[8 * dst:8 * dst + 8]
-
-    ucopies = [remote(u.at[1, pl.ds(48 * n, 48)], ur.at[pl.ds(48 * n, 48)], u_s.at[n], u_r.at[n], gx, partner)
-               for n in range(4)]
-    for copy in ucopies:
-        copy.start()
+                u[dst, 16 * k + 8 * part:16 * k + 8 * part + 8, :] = v[8 * dst:8 * dst + 8]
+        if k % 3 == 2:
+            ucopies[k // 3].start()
 
     zero8 = jnp.zeros((8, 128), F32)
 
-    def finish(v, hh, yy):
+    def finish(v, hh, yy, act):
         hi, lo = hilo(jnp.concatenate([v, zero8], 0))
         r = mm(jnp.concatenate([hi, hi, lo], 0), tzi_v[...], (((0,), (0,)), ((), ())))
         for yp in range(2):
-            rows = pl.ds(pl.multiple_of((2 * yy + yp) * 128 + hh * 64, 64), 64)
-            v_out[rows, :] = v_out[rows, :] + r[64 * yp:64 * yp + 64]
+            yr = 2 * yy + yp
+            t = r[64 * yp:64 * yp + 64] + co[pl.ds(pl.multiple_of(yr * 128 + hh * 64, 64), 64), :]
+            t = gelu(t) if act else t
+            for c in range(8):
+                v_out[pl.ds(hh * 1024 + c * 128 + yr, 8, stride=16), :] = t[8 * c:8 * c + 8]
 
     for yy in range(8):
-        finish(u[0, 24 * yy:24 * yy + 24, :], s, yy)
+        finish(u[0, pl.ds(yy, 24, stride=8), :], s, yy, True)
+    for copy in ucopies:
+        copy.wait_recv()
     for yy in range(8):
-        if yy % 2 == 0:
-            ucopies[yy // 2].wait_recv()
-        finish(ur[24 * yy:24 * yy + 24, :], 1 - s, yy)
+        finish(ur[pl.ds(yy, 24, stride=8), :], 1 - s, yy, False)
 
     for copy in acopies + ucopies + halos + ycopies + dcopies:
         copy.wait_send()
 
-    def w_done(m, carry):
-        d, slot, p, copy = w_copy(m)
-
-        @pl.when(d != me)
+    for mine, slot, p, copy in wcopies:
+        @pl.when(jnp.logical_not(mine))
         def _():
             copy.wait_send()
-        return carry
-
-    lax.fori_loop(0, 27, w_done, 0)
+
     part = rb.at[pl.ds(0, 63)]
     pltpu.make_async_copy(part, part, b_s).wait()
     pltpu.make_async_copy(part, part, c_s).wait()
 
 
 def gelu_kernel(v, out_hbm, outv, sem):
-    copies = []
+    s = lax.axis_index("gy") % 2
+    ready = pl.ds(pl.multiple_of(s * 1024, 1024), 1024)
+    copies = [pltpu.make_async_copy(v.at[ready], out_hbm.at[ready], sem.at[4])]
+    copies[0].start()
     for n in range(4):
-        for yr in range(16):
-            t = gelu(v[yr * 128 + 32 * n:yr * 128 + 32 * n + 32, :])
-            for c in range(4):
-                outv[pl.ds((4 * n + c) * 128 + yr, 8, stride=16), :] = t[8 * c:8 * c + 8]
-        rows = pl.ds(512 * n, 512)
-        copy = pltpu.make_async_copy(outv.at[rows], out_hbm.at[rows], sem.at[n])
+        start = pl.multiple_of((1 - s) * 1024 + 256 * n, 256)
+        for m in range(4):
+            outv[pl.ds(256 * n + 64 * m, 64), :] = gelu(v[pl.ds(start + 64 * m, 64), :])
+        copy = pltpu.make_async_copy(outv.at[pl.ds(256 * n, 256)], out_hbm.at[pl.ds(start, 256)], sem.at[n])
         copy.start()
         copies.append(copy)
     for copy in copies:
@@ -529,13 +555,13 @@
         vm((24, 384), BF16), vm((96, 128), BF16), vm((2, 16, 24, 128), F32), vm((256, 256), BF16), vm((256, 256), BF16),
         vm((256, 128), BF16), vm((2, 256, 128), BF16), vm((3, 8, 128), F32), vm((3, 8, 128), F32), vm((32, 27), F32),
         vm((96, 96), BF16), vm((64, 192), BF16),
-        vm((27, 4, 128), F32), vm((2, 24, 4, 128), F32), vm((512, 18 * 128), BF16), vm((1152, 512), BF16),
+        vm((27, 4, 128), F32), vm((2, 24, 4, 128), F32), vm((2, 2, 24, 256), F32), vm((512, 18 * 128), BF16), vm((1152, 512), BF16),
         vm((3, 512, 128), F32),
         vm((2, 128, 128), F32), vm((2, 128, 128), F32), vm((2, 16, 16, 128), F32), vm((4, 16, 128), F32),
         vm((4, 16, 128), F32), vm((2, 192, 128), F32), vm((192, 128), F32), vm((288, 128), F32), vm((3, 72, 128), F32),
         vm((73, 1, 128), F32), vm((64, 2, 1, 128), F32), vm((32, 2, 1, 128), F32), vm((64, 2, 1, 128), F32),
-        vm((4, 96, 128), F32), vm((2, 192, 128), F32), vm((192, 128), F32),
-        dma((15,)), dma((4,)), dma((4,)), dma((8,)), dma((8,)), dma((3,)), dma((3,)), dma, dma, dma, dma,
+        vm((4, 96, 128), F32), vm((2, 192, 128), F32), vm((192, 128), F32), vm((2048, 128), F32),
+        dma((16,)), dma((4,)), dma((4,)), dma((8,)), dma((8,)), dma((3,)), dma((3,)), dma, dma, dma, dma,
         dma((3,)), dma((4,)), dma((27,)), dma((2,)), dma((4,)), dma((4,)),
     ]
     any_spec = pl.BlockSpec(memory_space=pl.ANY)
@@ -556,7 +582,7 @@
         out_shape=jax.ShapeDtypeStruct((2048, 128), F32),
         in_specs=[vmem_spec],
         out_specs=any_spec,
-        scratch_shapes=[vm((2048, 128), F32), dma((4,))],
+        scratch_shapes=[vm((1024, 128), F32), dma((5,))],
         compiler_params=pltpu.CompilerParams(vmem_limit_bytes=8 * 1024 * 1024),
         name="act",
     )(v)

time: 42.4 us -> 40.6 us (0.958)
  Pallas kernels: 42.3 us -> 40.5 us
    pallas_call x1, Pallas kernels: 40.4 us -> 39.3 us  [shards(): pl.pallas_call(kernel, out_shape=jax.ShapeDtypeStruct((2048, 128), F32),...]
    pallas_call x1, Pallas kernels: 1.88 us -> 1.22 us  [shards(): pl.pallas_call(gelu_kernel, out_shape=jax.ShapeDtypeStruct((2048, 128), F...]
where the time goes in v3:
time: 40.6 us; the launch traced here: 40.5 us
  Pallas kernels  40.5 us (100%)
    pallas_call x1, Pallas kernels, shards(): pl.pallas_call(kernel, out_shape=jax.ShapeDtypeStruct((2048, 128), F32),...  39.3 us
    pallas_call x1, Pallas kernels, shards(): pl.pallas_call(gelu_kernel, out_shape=jax.ShapeDtypeStruct((2048, 128), F...  1.22 us

profile of v3, /device:TPU:1, one launch (start us, length us, event | category | flops | bytes accessed | tf_op | source)
XLA Modules:
  0.0 40.5 jit_solution(1889955740887590527)
XLA Ops:
  0.0 39.3 %layer.1.v = f32[2048,128]{1,0:T(8,128)S(1)} custom-call(f32[2048,128]{1,0:T(8,128)} %bitcast.7, f32[16,128,128]{2,1,0:T(8,128)} %bitcast.8, f32[512,27]{1,0:T(8,128)} %bitcast.9, f32[256,27]{1,0:T(8,128)} %bitcast.10, bf16[24,384]{1,0:T(8,128)(2,1)} %constant.24.clone.tzf, bf16[96,128]{1,0:T(8,128)(2,1)} %constant.25.clone.tzi, ...), custom_call_target="tpu_custom_call" | custom-call | tf_op jit(solution)/shard_map/layer/pallas_call | solution.py:570
  39.3 1.2 %act.1 = f32[2048,128]{1,0:T(8,128)} custom-call(f32[2048,128]{1,0:T(8,128)S(1)} %layer.1.v), custom_call_target="tpu_custom_call" | custom-call | tf_op jit(solution)/shard_map/act/pallas_call | solution.py:580

commit v4 on v3

--- a/solution.py
+++ b/solution.py
@@ -240,6 +240,8 @@
     copies[15].wait()
     part(s)
 
+    for n, (x0, y0) in enumerate(((0, 0), (0, 15), (7, 0), (7, 15))):
+        cs[n] = jnp.concatenate([fv[pl.ds(c * 128 + x0 * 16 + y0, 1), :] for c in range(16)], 0)
     @pl.when(jj != 3)
     def _():
         halos[2].start()
@@ -301,19 +303,7 @@
         copy.start()
         ycopies.append(copy)
 
-    @pl.when(jj == 3)
-    def _():
-        halos[2].start()
-
-    @pl.when(jj == 0)
-    def _():
-        halos[3].start()
-
-    for n, (x0, y0) in enumerate(((0, 0), (0, 15), (7, 0), (7, 15))):
-        cs[n] = jnp.concatenate([fv[pl.ds(c * 128 + x0 * 16 + y0, 1), :] for c in range(16)], 0)
     rs[72] = jnp.zeros((1, 128), F32)
-    for copy in halos[4:]:
-        copy.start()
 
 
     for copy in ycopies:
@@ -334,6 +324,17 @@
     src, _, _ = b_copy(gx, jj)
     pltpu.make_async_copy(src, rb.at[me], b_r).start()
     double = me % 8 == 0
+
+    @pl.when(jj == 3)
+    def _():
+        halos[2].start()
+
+    @pl.when(jj == 0)
+    def _():
+        halos[3].start()
+
+    for copy in halos[4:]:
+        copy.start()
 
     for n in (2, 10, 11, 12, 13):
         copies[n].wait()

time: 40.6 us -> 39 us (0.961)
  Pallas kernels: 40.5 us -> 38.9 us
    pallas_call x1, Pallas kernels: 39.3 us -> 37.7 us  [shards(): pl.pallas_call(kernel, out_shape=jax.ShapeDtypeStruct((2048, 128), F32),...]
where the time goes in v4:
time: 39 us; the launch traced here: 38.9 us
  Pallas kernels  38.9 us (100%)
    pallas_call x1, Pallas kernels, shards(): pl.pallas_call(kernel, out_shape=jax.ShapeDtypeStruct((2048, 128), F32),...  37.7 us
    pallas_call x1, Pallas kernels, shards(): pl.pallas_call(gelu_kernel, out_shape=jax.ShapeDtypeStruct((2048, 128), F...  1.22 us

profile of v4, /device:TPU:1, one launch (start us, length us, event | category | flops | bytes accessed | tf_op | source)
XLA Modules:
  0.0 38.9 jit_solution(981412024376174770)
XLA Ops:
  0.0 37.7 %layer.1.v = f32[2048,128]{1,0:T(8,128)S(1)} custom-call(f32[2048,128]{1,0:T(8,128)} %bitcast.7, f32[16,128,128]{2,1,0:T(8,128)} %bitcast.8, f32[512,27]{1,0:T(8,128)} %bitcast.9, f32[256,27]{1,0:T(8,128)} %bitcast.10, bf16[24,384]{1,0:T(8,128)(2,1)} %constant.24.clone.tzf, bf16[96,128]{1,0:T(8,128)(2,1)} %constant.25.clone.tzi, ...), custom_call_target="tpu_custom_call" | custom-call | tf_op jit(solution)/shard_map/layer/pallas_call | solution.py:571
  37.7 1.2 %act.1 = f32[2048,128]{1,0:T(8,128)} custom-call(f32[2048,128]{1,0:T(8,128)S(1)} %layer.1.v), custom_call_target="tpu_custom_call" | custom-call | tf_op jit(solution)/shard_map/act/pallas_call | solution.py:581

commit v5 on v4

--- a/solution.py
+++ b/solution.py
@@ -420,14 +420,23 @@
         hi, lo = hilo(jnp.concatenate(prods, 0))
         mx = mm(jnp.concatenate([hi, lo], 0), e2_v[...])
         mx = mx[0:size] + mx[size:2 * size]
-        for g in range(16):
-            for core in range(2):
-                for n, slot in enumerate(slots):
-                    lanes = slice(128 * core, 128 * core + 128)
-                    row = tx_v[0, g] * mx[48 * n:48 * n + 24, lanes] + tx_v[1, g] * mx[48 * n + 24:48 * n + 48, lanes]
-                    co_s[2 * g + core, slot] = jnp.sum(row, axis=0, keepdims=True)
-                if len(slots) == 1:
-                    co_s[2 * g + core, 1] = jnp.zeros((1, 128), F32)
+        for dz in (4, 3, 1, 2):
+            for nx, dx in enumerate(FAR_X):
+                g = ((z + dz) % 4) * 4 + xs4[nx]
+                for core in range(2):
+                    for n, slot in enumerate(slots):
+                        lanes = slice(128 * core, 128 * core + 128)
+                        row = tx_v[0, g] * mx[48 * n:48 * n + 24, lanes] + tx_v[1, g] * mx[48 * n + 24:48 * n + 48, lanes]
+                        co_s[2 * g + core, slot] = jnp.sum(row, axis=0, keepdims=True)
+                    if len(slots) == 1:
+                        co_s[2 * g + core, 1] = jnp.zeros((1, 128), F32)
+                for zd in ((dz, (dz + 4) % 8) if dz != 3 else (3, 7)):
+                    zz = (z + zd) % 8
+                    for dc in (1, 0):
+                        if zd or dx or dc:
+                            pj = (zz // 4) * 2 + (s + dc) % 2
+                            remote(co_s.at[2 * g + pj % 2], rc.at[me], c_s, c_r, g, 4 * y + pj).start()
+        pltpu.make_async_copy(co_s.at[2 * gx + s], rc.at[me], c_r).start()
 
     @pl.when(double)
     def _():
@@ -437,9 +446,6 @@
     def _():
         mix((0,))
 
-    for px, pj in peers:
-        remote(co_s.at[2 * px + pj % 2], rc.at[me], c_s, c_r, px, 4 * y + pj).start()
-    pltpu.make_async_copy(co_s.at[2 * gx + s], rc.at[me], c_r).start()
 
     b[384:512, :] = jnp.zeros((128, 18 * 128), BF16)
     for copy in halos:
@@ -512,7 +518,7 @@
     for copy in ucopies:
         copy.wait_recv()
     for yy in range(8):
-        finish(ur[pl.ds(yy, 24, stride=8), :], 1 - s, yy, False)
+        finish(ur[pl.ds(yy, 24, stride=8), :], 1 - s, yy, True)
 
     for copy in acopies + ucopies + halos + ycopies + dcopies:
         copy.wait_send()
@@ -527,18 +533,11 @@
     pltpu.make_async_copy(part, part, c_s).wait()
 
 
-def gelu_kernel(v, out_hbm, outv, sem):
-    s = lax.axis_index("gy") % 2
-    ready = pl.ds(pl.multiple_of(s * 1024, 1024), 1024)
-    copies = [pltpu.make_async_copy(v.at[ready], out_hbm.at[ready], sem.at[4])]
-    copies[0].start()
-    for n in range(4):
-        start = pl.multiple_of((1 - s) * 1024 + 256 * n, 256)
-        for m in range(4):
-            outv[pl.ds(256 * n + 64 * m, 64), :] = gelu(v[pl.ds(start + 64 * m, 64), :])
-        copy = pltpu.make_async_copy(outv.at[pl.ds(256 * n, 256)], out_hbm.at[pl.ds(start, 256)], sem.at[n])
+def copy_kernel(v, out_hbm, sem):
+    copies = [pltpu.make_async_copy(v.at[pl.ds(512 * n, 512)], out_hbm.at[pl.ds(512 * n, 512)], sem.at[n])
+              for n in range(4)]
+    for copy in copies:
         copy.start()
-        copies.append(copy)
     for copy in copies:
         copy.wait()
 
@@ -579,11 +578,11 @@
         name="layer",
     )(*[pltpu.with_memory_space_constraint(a, pltpu.HBM) for a in (f2, f3, w, cw, *consts)])
     out = pl.pallas_call(
-        gelu_kernel,
+        copy_kernel,
         out_shape=jax.ShapeDtypeStruct((2048, 128), F32),
         in_specs=[vmem_spec],
         out_specs=any_spec,
-        scratch_shapes=[vm((1024, 128), F32), dma((5,))],
+        scratch_shapes=[dma((4,))],
         compiler_params=pltpu.CompilerParams(vmem_limit_bytes=8 * 1024 * 1024),
         name="act",
     )(v)

time: 39 us -> 39 us (level)
  no operation moved by 1% of the time
where the time goes in v5:
time: 39 us; the launch traced here: 38.9 us
  Pallas kernels  38.9 us (100%)
    pallas_call x1, Pallas kernels, shards(): pl.pallas_call(kernel, out_shape=jax.ShapeDtypeStruct((2048, 128), F32),...  37.9 us
    pallas_call x1, Pallas kernels, shards(): pl.pallas_call(copy_kernel, out_shape=jax.ShapeDtypeStruct((2048, 128), F...  1 us

profile of v5, /device:TPU:1, one launch (start us, length us, event | category | flops | bytes accessed | tf_op | source)
XLA Modules:
  0.0 38.9 jit_solution(6195004572128367677)
XLA Ops:
  0.0 37.9 %layer.1.v = f32[2048,128]{1,0:T(8,128)S(1)} custom-call(f32[2048,128]{1,0:T(8,128)} %bitcast.7, f32[16,128,128]{2,1,0:T(8,128)} %bitcast.8, f32[512,27]{1,0:T(8,128)} %bitcast.9, f32[256,27]{1,0:T(8,128)} %bitcast.10, bf16[24,384]{1,0:T(8,128)(2,1)} %constant.24.clone.tzf, bf16[96,128]{1,0:T(8,128)(2,1)} %constant.25.clone.tzi, ...), custom_call_target="tpu_custom_call" | custom-call | tf_op jit(solution)/shard_map/layer/pallas_call | solution.py:570
  37.9 1.0 %act.1 = f32[2048,128]{1,0:T(8,128)} custom-call(f32[2048,128]{1,0:T(8,128)S(1)} %layer.1.v), custom_call_target="tpu_custom_call" | custom-call | tf_op jit(solution)/shard_map/act/pallas_call | solution.py:580

commit v6 on v5

--- a/solution.py
+++ b/solution.py
@@ -518,7 +518,7 @@
     for copy in ucopies:
         copy.wait_recv()
     for yy in range(8):
-        finish(ur[pl.ds(yy, 24, stride=8), :], 1 - s, yy, True)
+        finish(ur[pl.ds(yy, 24, stride=8), :], 1 - s, yy, False)
 
     for copy in acopies + ucopies + halos + ycopies + dcopies:
         copy.wait_send()
@@ -533,11 +533,18 @@
     pltpu.make_async_copy(part, part, c_s).wait()
 
 
-def copy_kernel(v, out_hbm, sem):
-    copies = [pltpu.make_async_copy(v.at[pl.ds(512 * n, 512)], out_hbm.at[pl.ds(512 * n, 512)], sem.at[n])
-              for n in range(4)]
-    for copy in copies:
+def gelu_kernel(v, out_hbm, outv, sem):
+    s = lax.axis_index("gy") % 2
+    ready = pl.ds(pl.multiple_of(s * 1024, 1024), 1024)
+    copies = [pltpu.make_async_copy(v.at[ready], out_hbm.at[ready], sem.at[4])]
+    copies[0].start()
+    for n in range(4):
+        start = pl.multiple_of((1 - s) * 1024 + 256 * n, 256)
+        for m in range(4):
+            outv[pl.ds(256 * n + 64 * m, 64), :] = gelu(v[pl.ds(start + 64 * m, 64), :])
+        copy = pltpu.make_async_copy(outv.at[pl.ds(256 * n, 256)], out_hbm.at[pl.ds(start, 256)], sem.at[n])
         copy.start()
+        copies.append(copy)
     for copy in copies:
         copy.wait()
 
@@ -578,11 +585,11 @@
         name="layer",
     )(*[pltpu.with_memory_space_constraint(a, pltpu.HBM) for a in (f2, f3, w, cw, *consts)])
     out = pl.pallas_call(
-        copy_kernel,
+        gelu_kernel,
         out_shape=jax.ShapeDtypeStruct((2048, 128), F32),
         in_specs=[vmem_spec],
         out_specs=any_spec,
-        scratch_shapes=[dma((4,))],
+        scratch_shapes=[vm((1024, 128), F32), dma((5,))],
         compiler_params=pltpu.CompilerParams(vmem_limit_bytes=8 * 1024 * 1024),
         name="act",
     )(v)

time: 39 us -> 38.9 us (level)
    pallas_call x1, Pallas kernels: 37.9 us -> 37.5 us  [shards(): pl.pallas_call(kernel, out_shape=jax.ShapeDtypeStruct((2048, 128), F32),...]
where the time goes in v6:
time: 38.9 us; the launch traced here: 38.8 us
  Pallas kernels  38.8 us (100%)
    pallas_call x1, Pallas kernels, shards(): pl.pallas_call(kernel, out_shape=jax.ShapeDtypeStruct((2048, 128), F32),...  37.5 us
    pallas_call x1, Pallas kernels, shards(): pl.pallas_call(gelu_kernel, out_shape=jax.ShapeDtypeStruct((2048, 128), F...  1.22 us

profile of v6, /device:TPU:1, one launch (start us, length us, event | category | flops | bytes accessed | tf_op | source)
XLA Modules:
  0.0 38.8 jit_solution(12847970874651145737)
XLA Ops:
  0.0 37.5 %layer.1.v = f32[2048,128]{1,0:T(8,128)S(1)} custom-call(f32[2048,128]{1,0:T(8,128)} %bitcast.7, f32[16,128,128]{2,1,0:T(8,128)} %bitcast.8, f32[512,27]{1,0:T(8,128)} %bitcast.9, f32[256,27]{1,0:T(8,128)} %bitcast.10, bf16[24,384]{1,0:T(8,128)(2,1)} %constant.24.clone.tzf, bf16[96,128]{1,0:T(8,128)(2,1)} %constant.25.clone.tzi, ...), custom_call_target="tpu_custom_call" | custom-call | tf_op jit(solution)/shard_map/layer/pallas_call | solution.py:577
  37.5 1.2 %act.1 = f32[2048,128]{1,0:T(8,128)} custom-call(f32[2048,128]{1,0:T(8,128)S(1)} %layer.1.v), custom_call_target="tpu_custom_call" | custom-call | tf_op jit(solution)/shard_map/act/pallas_call | solution.py:587
